TPU v7x, 512 devices: a whole 4x8x8 slice. The times are simulated.
512 devices in a mesh: row: 32 (over y_lo, x, core), col: 16 (over z, y_hi).
Axes of the slice: x: 4, y: 8 (y_hi: 2, y_lo: 4; y = y_hi * 4 + y_lo), z: 8, core: 2. Of those that a mesh axis runs over, the one named last changes fastest.
Arguments:
- features: bfloat16 [98304, 256], P(('row', 'col')), may hold values from -6 to 6
- weight: bfloat16 [256, 256], replicated, may hold values from -0.375 to 0.375
- tiles: bfloat16 [32, 16, 256, 64, 128], P('row', 'col'), may hold values from -0.0546875 to 0.0546875
- tile_rows: int32 [32, 16, 512], P('row', 'col'), may hold values from 0 to 47
- tile_cols: int32 [32, 16, 512], P('row', 'col'), may hold values from 0 to 95
- counts: int32 [32, 16], P('row', 'col'), may hold values from 128 to 512, as said below
Outputs:
- output: bfloat16 [98304, 256], P(('row', 'col'))
Inputs may be any that keep to these rules, and one draw needn't show every extreme that they name: `counts`: some grid cell has exactly 512 live slots.
All inputs are finite; a program needn't handle non-finite values.
Results may differ from a plain program's by a relative error of at most 0.0049.
Values may be sent and summed in bfloat16 or wider, within the bound.
No kernel may reach another device: no remote copies, remote signals or barrier semaphores. Data moves between devices by JAX's collectives and lax.ppermute only.
A program may use at most 64 MiB of HBM per device.

v0:
```python
import jax
import jax.numpy as jnp
from jax import lax
from jax.sharding import PartitionSpec as P

TILE = 64


def body(features, weight, tiles, tile_rows, tile_cols, counts):
    feature_width = weight.shape[1]
    product_rows = jnp.dot(features, weight, preferred_element_type=jnp.float32).astype(
        jnp.bfloat16
    )
    gathered = lax.all_gather(product_rows, "row", axis=0, tiled=True)
    column_table = gathered.reshape(gathered.shape[0] // TILE, TILE, feature_width)
    row_tiles = lax.axis_size("col") * features.shape[0] // TILE
    slot_count = tile_rows.shape[2]
    block_size = min(64, slot_count)
    half_block = block_size // 2
    passes = slot_count // block_size
    pair_list = tiles[0, 0]
    row_list = tile_rows[0, 0]
    col_list = tile_cols[0, 0]
    live_count = counts[0, 0]
    block_slots = jnp.arange(block_size, dtype=jnp.int32)

    def add_block(block_index, total):
        first = block_index * block_size
        pair_block = lax.dynamic_slice_in_dim(pair_list, block_index * half_block, half_block, 0)
        pair_block = pair_block.reshape(half_block, TILE, 2, TILE)
        row_block = lax.dynamic_slice_in_dim(row_list, first, block_size, 0)
        col_block = lax.dynamic_slice_in_dim(col_list, first, block_size, 0)
        picked = column_table[col_block].reshape(half_block, 2, TILE, feature_width)
        terms = jnp.einsum(
            "qajb,qjbf->qjaf", pair_block, picked, preferred_element_type=jnp.float32
        )
        terms = terms.reshape(block_size, TILE, feature_width)
        in_use = (first + block_slots < live_count).astype(jnp.float32)
        terms = terms * in_use[:, None, None]
        return total.at[row_block].add(terms)

    zero_total = jnp.zeros((row_tiles, TILE, feature_width), jnp.float32)
    total = lax.fori_loop(0, passes, add_block, zero_total)
    partial_value = total.reshape(row_tiles * TILE, feature_width)
    own_rows = lax.psum_scatter(partial_value, "col", scatter_dimension=0, tiled=True)
    return jnp.maximum(own_rows, 0.0).astype(jnp.bfloat16)


def solution(mesh):
    return jax.shard_map(
        body,
        mesh=mesh,
        in_specs=(
            P(("row", "col"), None),
            P(),
            P("row", "col", None, None, None),
            P("row", "col", None),
            P("row", "col", None),
            P("row", "col"),
        ),
        out_specs=P(("row", "col"), None),
        check_vma=False,
    )
```

profile of v0, /device:TPU:8, one launch (start us, length us, event | category | flops | bytes accessed | tf_op | source)
XLA Modules:
  0.0 513.0 jit_solution(17624238361777435077)
XLA Ops:
  6.5 0.9 copy-done
  7.4 1.7 convolution_convert_fusion
  9.2 68.8 %all-gather.2.cloned.1.call-done = bf16[6144,256]{1,0:T(8,128)(2,1)} async-done(((bf16[192,256]{1,0:T(8,128)(2,1)}), bf16[6144,256]{1,0:T(8,128)(2,1)}) %all-gather.2.cloned.1.call-update) | async-done | bytes 3145744 | tf_op jit(solution)/shard_map/all_gather | solution.py:14
  78.4 195.1 %while.14 = (s32[]{:T(128)}, f32[48,64,256]{2,1,0:T(8,128)S(1)}, s32[512]{0:T(512)}, bf16[256,64,128]{2,1,0:T(8,128)(2,1)}, s32[512]{0:T(512)}, /*index=5*/bf16[...) while((s32[]{:T(128)}, f32[48,64,256]{2,1,0:T(8,128)S(1)}, ...), condition=%wide.region_2.0_spmd.clone, body=%wide.region_0.0_spmd.clone.sunk | while | flops 136316496 | bytes 34085360 | solution.py:43
  78.4 0.7 compare_convert_fusion.2
  79.1 0.8 compare_select_fusion.3
  79.8 1.9 constant_dynamic-slice_fusion.2
  81.7 3.2 reshape.70
  84.9 3.9 gather_fusion
  88.8 2.6 fusion.12
  91.4 2.5 bitcast_multiply_fusion.2
  93.9 8.8 %scatter_fusion = f32[48,64,256]{2,1,0:T(8,128)S(1)} fusion(f32[48,64,256]{2,1,0:T(8,128)S(1)} %get-tuple-element.238, s32[64]{0:T(128)S(1)} %get-tuple-element.222, f32[64,64,256]{2,1,0:T(8,128)} %bitcast_multiply_fusion.2), kind=kCustom, calls=%fused_computation.1.clone.clone.1 | custom fusion | flops 1048576 | bytes 12583168 | tf_op jit(solution)/shard_map/while/body/eval_jaxpr/scatter-add | solution.py:40
  103.4 0.8 compare_select_fusion.3
  104.2 1.9 constant_dynamic-slice_fusion.2
  106.1 3.2 reshape.70
  109.3 3.9 gather_fusion
  113.2 2.6 fusion.12
  115.8 2.5 bitcast_multiply_fusion.2
  118.3 8.8 %scatter_fusion = f32[48,64,256]{2,1,0:T(8,128)S(1)} fusion(f32[48,64,256]{2,1,0:T(8,128)S(1)} %get-tuple-element.238, s32[64]{0:T(128)S(1)} %get-tuple-element.222, f32[64,64,256]{2,1,0:T(8,128)} %bitcast_multiply_fusion.2), kind=kCustom, calls=%fused_computation.1.clone.clone.1 | custom fusion | flops 1048576 | bytes 12583168 | tf_op jit(solution)/shard_map/while/body/eval_jaxpr/scatter-add | solution.py:40
  127.8 0.8 compare_select_fusion.3
  128.6 1.9 constant_dynamic-slice_fusion.2
  130.5 3.2 reshape.70
  133.7 3.9 gather_fusion
  137.6 2.6 fusion.12
  140.2 2.5 bitcast_multiply_fusion.2
  142.7 8.8 %scatter_fusion = f32[48,64,256]{2,1,0:T(8,128)S(1)} fusion(f32[48,64,256]{2,1,0:T(8,128)S(1)} %get-tuple-element.238, s32[64]{0:T(128)S(1)} %get-tuple-element.222, f32[64,64,256]{2,1,0:T(8,128)} %bitcast_multiply_fusion.2), kind=kCustom, calls=%fused_computation.1.clone.clone.1 | custom fusion | flops 1048576 | bytes 12583168 | tf_op jit(solution)/shard_map/while/body/eval_jaxpr/scatter-add | solution.py:40
  152.2 0.8 compare_select_fusion.3
  153.0 1.9 constant_dynamic-slice_fusion.2
  154.9 3.2 reshape.70
  158.1 3.9 gather_fusion
  162.0 2.6 fusion.12
  164.6 2.5 bitcast_multiply_fusion.2
  167.1 8.8 %scatter_fusion = f32[48,64,256]{2,1,0:T(8,128)S(1)} fusion(f32[48,64,256]{2,1,0:T(8,128)S(1)} %get-tuple-element.238, s32[64]{0:T(128)S(1)} %get-tuple-element.222, f32[64,64,256]{2,1,0:T(8,128)} %bitcast_multiply_fusion.2), kind=kCustom, calls=%fused_computation.1.clone.clone.1 | custom fusion | flops 1048576 | bytes 12583168 | tf_op jit(solution)/shard_map/while/body/eval_jaxpr/scatter-add | solution.py:40
  176.6 0.8 compare_select_fusion.3
  177.4 1.9 constant_dynamic-slice_fusion.2
  179.3 3.2 reshape.70
  182.5 3.9 gather_fusion
  186.4 2.6 fusion.12
  189.0 2.5 bitcast_multiply_fusion.2
  191.5 8.8 %scatter_fusion = f32[48,64,256]{2,1,0:T(8,128)S(1)} fusion(f32[48,64,256]{2,1,0:T(8,128)S(1)} %get-tuple-element.238, s32[64]{0:T(128)S(1)} %get-tuple-element.222, f32[64,64,256]{2,1,0:T(8,128)} %bitcast_multiply_fusion.2), kind=kCustom, calls=%fused_computation.1.clone.clone.1 | custom fusion | flops 1048576 | bytes 12583168 | tf_op jit(solution)/shard_map/while/body/eval_jaxpr/scatter-add | solution.py:40
  201.0 0.8 compare_select_fusion.3
  201.8 1.9 constant_dynamic-slice_fusion.2
  203.7 3.2 reshape.70
  206.9 3.9 gather_fusion
  210.8 2.6 fusion.12
  213.4 2.5 bitcast_multiply_fusion.2
  215.9 8.8 %scatter_fusion = f32[48,64,256]{2,1,0:T(8,128)S(1)} fusion(f32[48,64,256]{2,1,0:T(8,128)S(1)} %get-tuple-element.238, s32[64]{0:T(128)S(1)} %get-tuple-element.222, f32[64,64,256]{2,1,0:T(8,128)} %bitcast_multiply_fusion.2), kind=kCustom, calls=%fused_computation.1.clone.clone.1 | custom fusion | flops 1048576 | bytes 12583168 | tf_op jit(solution)/shard_map/while/body/eval_jaxpr/scatter-add | solution.py:40
  225.4 0.8 compare_select_fusion.3
  226.2 1.9 constant_dynamic-slice_fusion.2
  228.1 3.2 reshape.70
  231.3 3.9 gather_fusion
  235.2 2.6 fusion.12
  237.8 2.5 bitcast_multiply_fusion.2
  240.3 8.8 %scatter_fusion = f32[48,64,256]{2,1,0:T(8,128)S(1)} fusion(f32[48,64,256]{2,1,0:T(8,128)S(1)} %get-tuple-element.238, s32[64]{0:T(128)S(1)} %get-tuple-element.222, f32[64,64,256]{2,1,0:T(8,128)} %bitcast_multiply_fusion.2), kind=kCustom, calls=%fused_computation.1.clone.clone.1 | custom fusion | flops 1048576 | bytes 12583168 | tf_op jit(solution)/shard_map/while/body/eval_jaxpr/scatter-add | solution.py:40
  249.8 0.8 compare_select_fusion.3
  250.6 1.9 constant_dynamic-slice_fusion.2
  252.5 3.2 reshape.70
  255.6 3.9 gather_fusion
  259.5 2.6 fusion.12
  262.1 2.5 bitcast_multiply_fusion.2
  264.7 8.8 %scatter_fusion = f32[48,64,256]{2,1,0:T(8,128)S(1)} fusion(f32[48,64,256]{2,1,0:T(8,128)S(1)} %get-tuple-element.238, s32[64]{0:T(128)S(1)} %get-tuple-element.222, f32[64,64,256]{2,1,0:T(8,128)} %bitcast_multiply_fusion.2), kind=kCustom, calls=%fused_computation.1.clone.clone.1 | custom fusion | flops 1048576 | bytes 12583168 | tf_op jit(solution)/shard_map/while/body/eval_jaxpr/scatter-add | solution.py:40
  273.5 1.6 copy-done.1
  275.2 229.4 %reduce-scatter.2.cloned.1.call-done = f32[192,256]{1,0:T(8,128)} async-done(((f32[3072,256]{1,0:T(8,128)}), f32[192,256]{1,0:T(8,128)}) %reduce-scatter.2.cloned.1.call-update) | async-done | bytes 196624 | tf_op jit(solution)/shard_map/reduce_scatter | solution.py:45
  504.6 1.6 maximum_convert_fusion
  (22 shorter events, 5.0 us)
Async XLA Ops:
  6.5 0.9 copy-start
  6.5 71.5 %all-gather.2.cloned.1.call-start = ((), (), s32[]{:S(2)}) async-start(), calls=%async_computation.1 | async-start | bytes 3244032 | tf_op jit(solution)/shard_map/all_gather | solution.py:14
  9.2 495.4 %reduce-scatter.2.cloned.1.call-start = ((), (), s32[]{:S(2)}) async-start(), calls=%async_computation.2 | async-start | bytes 3342336 | tf_op jit(solution)/shard_map/reduce_scatter | solution.py:45
  273.5 1.6 copy-start.1
Sparse Core Ops, SparseCore 0:
  9.5 68.4 all-gather.1
  275.3 229.2 reduce-scatter.1
where the time goes:
time: 516 us; the launch traced here: 513 us
  waiting for transfers between devices  298 us (58%)
  other arithmetic  104 us (20%)
  local copies, waits for them, and re-layouts  74.5 us (14%)
  matrix products  22.5 us (4%)
  between operations  13.4 us (3%)
    reduce_scatter x1, waiting for transfers between devices, body(): lax.psum_scatter(partial_value, 'col', scatter_dimension=0, tiled=True)  229 us
    scatter-add x8, other arithmetic, add_block(): return total.at[row_block].add(terms)  70.4 us
    all_gather x1, waiting for transfers between devices, body(): gathered = lax.all_gather(product_rows, 'row', axis=0, tiled=True)  68.8 us
    gather x8, local copies, waits for them, and re-layouts, add_block(): picked = column_table[col_block].reshape(half_block, 2, TILE, feature_width)  31.2 us
    reshape x8, local copies, waits for them, and re-layouts, add_block(): pair_block = pair_block.reshape(half_block, TILE, 2, TILE)  25.5 us
    dot_general x8, matrix products, add_block(): jnp.einsum('qajb,qjbf->qjaf', pair_block, picked, preferred_element_type=...  20.8 us
    mul x8, other arithmetic, add_block(): terms = terms * in_use[:, None, None]  20.4 us
    dynamic_slice x8, local copies, waits for them, and re-layouts, add_block(): lax.dynamic_slice_in_dim(pair_list, block_index * half_block, half_block, 0)  14.9 us
  transfers between devices with their start and end apart: 2, of which 2 were waited for; matrix products, arithmetic and copies ran while one was open for 0% of the time, Pallas kernels for 0%

commit v1 on v0

v1 whole, which is shorter than its diff:
```python
import jax
import jax.numpy as jnp
from jax import lax
from jax.experimental import pallas as pl
from jax.experimental.pallas import tpu as pltpu
from jax.sharding import PartitionSpec as P

TILE = 64
Y_CHIPS, X_CHIPS, CORES = 4, 4, 2
UNROLL = 4
CHUNKS = 8


def row_shift(dy, dx, dcore):
    pairs = []
    for source in range(Y_CHIPS * X_CHIPS * CORES):
        y, x, core = source // (X_CHIPS * CORES), source // CORES % X_CHIPS, source % CORES
        y, x, core = (y + dy) % Y_CHIPS, (x + dx) % X_CHIPS, (core + dcore) % CORES
        pairs.append((source, (y * X_CHIPS + x) * CORES + core))
    return pairs


def shift(value, dy, dx, dcore):
    return lax.ppermute(value, "row", row_shift(dy, dx, dcore))


def spmm_kernel(rows, cols, live, *refs):
    parts, tiles_hbm, out, table, tiles, total, part_sem, tile_sem = refs[:8], *refs[8:]
    part_tiles = table.shape[0] // len(parts)
    pair_chunk = tiles.shape[0] // CHUNKS
    part_copies = [
        pltpu.make_async_copy(part, table.at[pl.ds(i * part_tiles, part_tiles)], part_sem.at[i])
        for i, part in enumerate(parts)
    ]
    tile_copies = [
        pltpu.make_async_copy(
            tiles_hbm.at[pl.ds(i * pair_chunk, pair_chunk)],
            tiles.at[pl.ds(i * pair_chunk, pair_chunk)],
            tile_sem.at[i],
        )
        for i in range(CHUNKS)
    ]
    for copy in part_copies + tile_copies:
        copy.start()
    total[...] = jnp.zeros_like(total)
    lane = lax.broadcasted_iota(jnp.int32, (TILE, 2 * TILE), 1)
    low = (lane < TILE).astype(jnp.bfloat16)
    high = (lane >= TILE).astype(jnp.bfloat16)
    for copy in part_copies:
        copy.wait()
    steps = (live[0] + 2 * UNROLL - 1) // (2 * UNROLL)
    chunk_steps = pair_chunk // UNROLL

    for chunk in range(CHUNKS):
        tile_copies[chunk].wait()

        def step(i, carry):
            first = (chunk * chunk_steps + i) * UNROLL
            terms = []
            for j in range(UNROLL):
                pair = first + j
                block = tiles[pair]
                left = jnp.concatenate([block * low, block * high], axis=0)
                right = jnp.concatenate([table[cols[2 * pair]], table[cols[2 * pair + 1]]], axis=0)
                terms.append(jnp.dot(left, right, preferred_element_type=jnp.float32))
            for j in range(UNROLL):
                pair = first + j
                total[rows[2 * pair]] += terms[j][:TILE]
                total[rows[2 * pair + 1]] += terms[j][TILE:]
            return carry

        lax.fori_loop(0, jnp.clip(steps - chunk * chunk_steps, 0, chunk_steps), step, 0)
    row_tiles = out.shape[0] // TILE
    out[...] = total[:row_tiles].reshape(out.shape).astype(out.dtype)


def body(features, weight, tiles, tile_rows, tile_cols, counts):
    own, width = features.shape
    slots = tile_rows.shape[2]
    n_col = lax.axis_size("col")
    row_tiles = n_col * own // TILE
    own_tiles = own // TILE
    me = lax.axis_index("row")
    my_y, my_x, my_core = me // (X_CHIPS * CORES), me // CORES % X_CHIPS, me % CORES

    product = jnp.dot(features, weight, preferred_element_type=jnp.float32).astype(jnp.bfloat16)
    column = jnp.concatenate([product] + [shift(product, k, 0, 0) for k in (1, 2, 3)], axis=0)
    near = [column, shift(column, 0, 1, 0), shift(column, 0, 3, 0), shift(column, 0, 2, 0)]
    far = [shift(v, 0, 0, 1) for v in near]
    parts = [v.reshape(-1, TILE, width) for v in near + far]

    live = counts[0]
    rows = jnp.where(jnp.arange(slots, dtype=jnp.int32) < live, tile_rows[0, 0], row_tiles)
    block, inner = tile_cols[0, 0] // own_tiles, tile_cols[0, 0] % own_tiles
    y, x, core = block // (X_CHIPS * CORES), block // CORES % X_CHIPS, block % CORES
    back_y, back_x = (my_y - y) % Y_CHIPS, (my_x - x) % X_CHIPS
    place_x = jnp.where(back_x >= 2, 5 - back_x, back_x)
    cols = (((core + my_core) % 2 * X_CHIPS + place_x) * Y_CHIPS + back_y) * own_tiles + inner

    scalar = pl.BlockSpec(memory_space=pltpu.SMEM)
    hbm = pl.BlockSpec(memory_space=pl.ANY)
    partial_rows = pl.pallas_call(
        spmm_kernel,
        out_shape=jax.ShapeDtypeStruct((row_tiles * TILE, width), jnp.bfloat16),
        in_specs=[scalar] * 3 + [hbm] * 9,
        out_specs=pl.BlockSpec(memory_space=pltpu.VMEM),
        scratch_shapes=[
            pltpu.VMEM((8 * parts[0].shape[0], TILE, width), jnp.bfloat16),
            pltpu.VMEM(tiles.shape[2:], jnp.bfloat16),
            pltpu.VMEM((row_tiles + 1, TILE, width), jnp.float32),
            pltpu.SemaphoreType.DMA((8,)),
            pltpu.SemaphoreType.DMA((CHUNKS,)),
        ],
        compiler_params=pltpu.CompilerParams(vmem_limit_bytes=32 << 20),
    )(rows, cols, live, *parts, tiles[0, 0])

    received = lax.all_to_all(partial_rows, "col", 0, 0, tiled=True)
    received = received.reshape(n_col, own, width).astype(jnp.float32)
    return jnp.maximum(jnp.sum(received, axis=0), 0.0).astype(jnp.bfloat16)


def solution(mesh):
    return jax.shard_map(
        body,
        mesh=mesh,
        in_specs=(
            P(("row", "col"), None),
            P(),
            P("row", "col", None, None, None),
            P("row", "col", None),
            P("row", "col", None),
            P("row", "col"),
        ),
        out_specs=P(("row", "col"), None),
        check_vma=False,
    )
```

time: 516 us -> 132 us (0.26)
  the two profiles are of different devices: /device:TPU:8 before, /device:TPU:22 now
where the time goes in v1:
time: 132 us; the launch traced here: 131 us
  blocking collectives  68.5 us (52%)
  starting transfers between devices  28.2 us (21%)
  Pallas kernels  14.8 us (11%)
  waiting for transfers between devices  11.8 us (9%)
  local copies, waits for them, and re-layouts  3.09 us (2%)
  other arithmetic  3.01 us (2%)
    all_to_all x1, blocking collectives, body(): received = lax.all_to_all(partial_rows, 'col', 0, 0, tiled=True)  68.5 us
    ppermute x10, starting transfers between devices, shift(): return lax.ppermute(value, 'row', row_shift(dy, dx, dcore))  28.2 us
    pallas_call x1, Pallas kernels, body(): pl.pallas_call(spmm_kernel, out_shape=jax.ShapeDtypeStruct((row_tiles * T...  14.8 us
    ppermute x10, waiting for transfers between devices, shift(): return lax.ppermute(value, 'row', row_shift(dy, dx, dcore))  11.8 us
    unnamed x4, local copies, waits for them, and re-layouts  3.09 us
  transfers between devices with their start and end apart: 10, of which 4 were waited for; matrix products, arithmetic and copies ran while one was open for 2% of the time, Pallas kernels for 0%

profile of v1, /device:TPU:22, one launch (start us, length us, event | category | flops | bytes accessed | tf_op | source)
XLA Modules:
  0.0 131.2 jit_solution(17257595587940920653)
XLA Ops:
  0.0 0.0 copy-start
  0.0 0.9 copy-done
  0.9 1.1 convolution_convert_fusion
  2.0 2.4 %collective-permute-start.2 = (bf16[192,256]{1,0:T(8,128)(2,1)S(1)}, bf16[192,256]{1,0:T(8,128)(2,1)S(1)}, u32[]{:S(2)}, u32[]{:S(2)}) collective-permute-start(bf16[192,256]{1,0:T(8,128)(2,1)S(1)} %convolution_convert_fusion), channel_id=1, source_target_pairs={{0,384},{16,400},{32,416},{48,432},{64,448},{80,464},{96,480},{112... | collective-permute-start | bytes 294920 | tf_op jit(solution)/shard_map/ppermute | solution.py:24
  4.3 5.4 %collective-permute-start.1 = (bf16[192,256]{1,0:T(8,128)(2,1)S(1)}, bf16[192,256]{1,0:T(8,128)(2,1)S(1)}, u32[]{:S(2)}, u32[]{:S(2)}) collective-permute-start(bf16[192,256]{1,0:T(8,128)(2,1)S(1)} %convolution_convert_fusion), channel_id=1, source_target_pairs={{0,256},{16,272},{32,288},{48,304},{64,320},{80,336},{96,352},{112... | collective-permute-start | bytes 294920 | tf_op jit(solution)/shard_map/ppermute | solution.py:24
  9.7 1.9 %collective-permute-start = (bf16[192,256]{1,0:T(8,128)(2,1)S(1)}, bf16[192,256]{1,0:T(8,128)(2,1)S(1)}, u32[]{:S(2)}, u32[]{:S(2)}) collective-permute-start(bf16[192,256]{1,0:T(8,128)(2,1)S(1)} %convolution_convert_fusion), channel_id=1, source_target_pairs={{0,128},{16,144},{32,160},{48,176},{64,192},{80,208},{96,224},{112... | collective-permute-start | bytes 294920 | tf_op jit(solution)/shard_map/ppermute | solution.py:24
  11.7 0.0 collective-permute-done.2
  11.7 0.9 collective-permute-done.1
  12.6 4.2 %collective-permute-done = bf16[192,256]{1,0:T(8,128)(2,1)S(1)} collective-permute-done((bf16[192,256]{1,0:T(8,128)(2,1)S(1)}, bf16[192,256]{1,0:T(8,128)(2,1)S(1)}, u32[]{:S(2)}, u32[]{:S(2)}) %collective-permute-start) | collective-permute-done | bytes 98336 | tf_op jit(solution)/shard_map/ppermute | solution.py:24
  16.8 3.3 %collective-permute-start.5 = (bf16[768,256]{1,0:T(8,128)(2,1)S(1)}, bf16[768,256]{1,0:T(8,128)(2,1)S(1)}, u32[]{:S(2)}, u32[]{:S(2)}) collective-permute-start(bf16[768,256]{1,0:T(8,128)(2,1)S(1)} %pad_maximum_fusion), channel_id=1, source_target_pairs={{0,64},{16,80},{32,96},{48,112},{64,0},{80,16},{96,32},{112,48},{1... | collective-permute-start | bytes 1179656 | tf_op jit(solution)/shard_map/ppermute | solution.py:24
  20.1 3.1 %collective-permute-start.4 = (bf16[768,256]{1,0:T(8,128)(2,1)S(1)}, bf16[768,256]{1,0:T(8,128)(2,1)S(1)}, u32[]{:S(2)}, u32[]{:S(2)}) collective-permute-start(bf16[768,256]{1,0:T(8,128)(2,1)S(1)} %pad_maximum_fusion), channel_id=1, source_target_pairs={{0,96},{16,112},{32,0},{48,16},{64,32},{80,48},{96,64},{112,80},{1... | collective-permute-start | bytes 1179656 | tf_op jit(solution)/shard_map/ppermute | solution.py:24
  23.2 3.9 %collective-permute-start.3 = (bf16[768,256]{1,0:T(8,128)(2,1)S(1)}, bf16[768,256]{1,0:T(8,128)(2,1)S(1)}, u32[]{:S(2)}, u32[]{:S(2)}) collective-permute-start(bf16[768,256]{1,0:T(8,128)(2,1)S(1)} %pad_maximum_fusion), channel_id=1, source_target_pairs={{0,32},{16,48},{32,64},{48,80},{64,96},{80,112},{96,0},{112,16},{1... | collective-permute-start | bytes 1179656 | tf_op jit(solution)/shard_map/ppermute | solution.py:24
  27.9 0.7 compare_reduce_fusion
  28.6 1.9 %collective-permute-start.6 = (bf16[768,256]{1,0:T(8,128)(2,1)S(1)}, bf16[768,256]{1,0:T(8,128)(2,1)S(1)}, u32[]{:S(2)}, u32[]{:S(2)}) collective-permute-start(bf16[768,256]{1,0:T(8,128)(2,1)S(1)} %pad_maximum_fusion), channel_id=1, source_target_pairs={{0,16},{16,0},{32,48},{48,32},{64,80},{80,64},{96,112},{112,96},{1... | collective-permute-start | bytes 1179656 | tf_op jit(solution)/shard_map/ppermute | solution.py:24
  30.5 1.8 %collective-permute-done.5 = bf16[768,256]{1,0:T(8,128)(2,1)S(1)} collective-permute-done((bf16[768,256]{1,0:T(8,128)(2,1)S(1)}, bf16[768,256]{1,0:T(8,128)(2,1)S(1)}, u32[]{:S(2)}, u32[]{:S(2)}) %collective-permute-start.5) | collective-permute-done | bytes 393248 | tf_op jit(solution)/shard_map/ppermute | solution.py:24
  32.3 1.9 %collective-permute-start.9 = (bf16[768,256]{1,0:T(8,128)(2,1)S(1)}, bf16[768,256]{1,0:T(8,128)(2,1)S(1)}, u32[]{:S(2)}, u32[]{:S(2)}) collective-permute-start(bf16[768,256]{1,0:T(8,128)(2,1)S(1)} %collective-permute-done.5), channel_id=1, source_target_pairs={{0,16},{16,0},{32,48},{48,32},{64,80},{80,64},{96,112},{112,96},{1... | collective-permute-start | bytes 1179656 | tf_op jit(solution)/shard_map/ppermute | solution.py:24
  34.2 4.9 %collective-permute-done.4 = bf16[768,256]{1,0:T(8,128)(2,1)S(1)} collective-permute-done((bf16[768,256]{1,0:T(8,128)(2,1)S(1)}, bf16[768,256]{1,0:T(8,128)(2,1)S(1)}, u32[]{:S(2)}, u32[]{:S(2)}) %collective-permute-start.4) | collective-permute-done | bytes 393248 | tf_op jit(solution)/shard_map/ppermute | solution.py:24
  39.1 1.9 %collective-permute-start.8 = (bf16[768,256]{1,0:T(8,128)(2,1)S(1)}, bf16[768,256]{1,0:T(8,128)(2,1)S(1)}, u32[]{:S(2)}, u32[]{:S(2)}) collective-permute-start(bf16[768,256]{1,0:T(8,128)(2,1)S(1)} %collective-permute-done.4), channel_id=1, source_target_pairs={{0,16},{16,0},{32,48},{48,32},{64,80},{80,64},{96,112},{112,96},{1... | collective-permute-start | bytes 1179656 | tf_op jit(solution)/shard_map/ppermute | solution.py:24
  41.1 0.0 collective-permute-done.3
  41.1 2.4 %collective-permute-start.7 = (bf16[768,256]{1,0:T(8,128)(2,1)S(1)}, bf16[768,256]{1,0:T(8,128)(2,1)S(1)}, u32[]{:S(2)}, u32[]{:S(2)}) collective-permute-start(bf16[768,256]{1,0:T(8,128)(2,1)S(1)} %collective-permute-done.3), channel_id=1, source_target_pairs={{0,16},{16,0},{32,48},{48,32},{64,80},{80,64},{96,112},{112,96},{1... | collective-permute-start | bytes 1179656 | tf_op jit(solution)/shard_map/ppermute | solution.py:24
  43.5 0.7 broadcast_divide_fusion
  44.2 0.7 fusion.7
  44.9 0.0 collective-permute-done.6
  44.9 0.0 collective-permute-done.9
  44.9 0.0 collective-permute-done.8
  44.9 0.0 collective-permute-done.7
  44.9 0.0 copy-start.1
  45.0 2.2 %copy-done.1 = bf16[1,1,256,64,128]{4,3,2,1,0:T(8,128)(2,1)S(1)} copy-done((bf16[1,1,256,64,128]{4,3,2,1,0:T(8,128)(2,1)S(1)}, bf16[1,1,256,64,128]{4,3,2,1,0:T(8,128)(2,1)}, u32[]{:S(2)}) %copy-start.1) | copy-done | bytes 4194328
  47.1 14.8 %shard_map.64 = bf16[3072,256]{1,0:T(8,128)(2,1)S(1)} custom-call(s32[512]{0:T(512)S(1)} %get-tuple-element.8.rows, s32[512]{0:T(512)S(1)} %get-tuple-element.7.cols, s32[1]{0:T(128)} %bitcast.18.live, bf16[12,64,256]{2,1,0:T(8,128)(2,1)S(1)} %bitcast.21, bf16[12,64,256]{2,1,0:T(8,128)(2,1)S(1)} %bitcast.24, bf16[12,64,256]{2,1,0:T(8,128)(2,1)S(1)} %bitcast.23, ...), custom_call_target="tpu_custom_call" | custom-call | tf_op jit(solution)/shard_map/pallas_call | solution.py:102
  61.9 68.5 %all_to_all.9 = bf16[16,192,256]{2,1,0:T(8,128)(2,1)S(1)} all-to-all(bf16[16,192,256]{2,1,0:T(8,128)(2,1)S(1)} %bitcast.19), channel_id=1, replica_groups=mesh['row'=32,'col'=16] {'col'}, dimensions={0} | all-to-all | bytes 3145728 | tf_op jit(solution)/shard_map/all_to_all | solution.py:117
  130.4 0.2 convert_reduce_fusion
  130.6 0.7 maximum_convert_fusion
  (1 shorter events, 0.0 us)
Async XLA Ops:
  0.0 0.9 copy-start
  2.0 9.7 %collective-permute-start.2 = (bf16[192,256]{1,0:T(8,128)(2,1)S(1)}, bf16[192,256]{1,0:T(8,128)(2,1)S(1)}, u32[]{:S(2)}, u32[]{:S(2)}) collective-permute-start(bf16[192,256]{1,0:T(8,128)(2,1)S(1)} %convolution_convert_fusion), channel_id=1, source_target_pairs={{0,384},{16,400},{32,416},{48,432},{64,448},{80,464},{96,480},{112... | collective-permute-start | bytes 294920 | tf_op jit(solution)/shard_map/ppermute | solution.py:24
  4.3 8.3 %collective-permute-start.1 = (bf16[192,256]{1,0:T(8,128)(2,1)S(1)}, bf16[192,256]{1,0:T(8,128)(2,1)S(1)}, u32[]{:S(2)}, u32[]{:S(2)}) collective-permute-start(bf16[192,256]{1,0:T(8,128)(2,1)S(1)} %convolution_convert_fusion), channel_id=1, source_target_pairs={{0,256},{16,272},{32,288},{48,304},{64,320},{80,336},{96,352},{112... | collective-permute-start | bytes 294920 | tf_op jit(solution)/shard_map/ppermute | solution.py:24
  9.7 7.0 %collective-permute-start = (bf16[192,256]{1,0:T(8,128)(2,1)S(1)}, bf16[192,256]{1,0:T(8,128)(2,1)S(1)}, u32[]{:S(2)}, u32[]{:S(2)}) collective-permute-start(bf16[192,256]{1,0:T(8,128)(2,1)S(1)} %convolution_convert_fusion), channel_id=1, source_target_pairs={{0,128},{16,144},{32,160},{48,176},{64,192},{80,208},{96,224},{112... | collective-permute-start | bytes 294920 | tf_op jit(solution)/shard_map/ppermute | solution.py:24
  16.8 15.5 %collective-permute-start.5 = (bf16[768,256]{1,0:T(8,128)(2,1)S(1)}, bf16[768,256]{1,0:T(8,128)(2,1)S(1)}, u32[]{:S(2)}, u32[]{:S(2)}) collective-permute-start(bf16[768,256]{1,0:T(8,128)(2,1)S(1)} %pad_maximum_fusion), channel_id=1, source_target_pairs={{0,64},{16,80},{32,96},{48,112},{64,0},{80,16},{96,32},{112,48},{1... | collective-permute-start | bytes 1179656 | tf_op jit(solution)/shard_map/ppermute | solution.py:24
  20.1 19.0 %collective-permute-start.4 = (bf16[768,256]{1,0:T(8,128)(2,1)S(1)}, bf16[768,256]{1,0:T(8,128)(2,1)S(1)}, u32[]{:S(2)}, u32[]{:S(2)}) collective-permute-start(bf16[768,256]{1,0:T(8,128)(2,1)S(1)} %pad_maximum_fusion), channel_id=1, source_target_pairs={{0,96},{16,112},{32,0},{48,16},{64,32},{80,48},{96,64},{112,80},{1... | collective-permute-start | bytes 1179656 | tf_op jit(solution)/shard_map/ppermute | solution.py:24
  23.2 17.8 %collective-permute-start.3 = (bf16[768,256]{1,0:T(8,128)(2,1)S(1)}, bf16[768,256]{1,0:T(8,128)(2,1)S(1)}, u32[]{:S(2)}, u32[]{:S(2)}) collective-permute-start(bf16[768,256]{1,0:T(8,128)(2,1)S(1)} %pad_maximum_fusion), channel_id=1, source_target_pairs={{0,32},{16,48},{32,64},{48,80},{64,96},{80,112},{96,0},{112,16},{1... | collective-permute-start | bytes 1179656 | tf_op jit(solution)/shard_map/ppermute | solution.py:24
  28.6 16.3 %collective-permute-start.6 = (bf16[768,256]{1,0:T(8,128)(2,1)S(1)}, bf16[768,256]{1,0:T(8,128)(2,1)S(1)}, u32[]{:S(2)}, u32[]{:S(2)}) collective-permute-start(bf16[768,256]{1,0:T(8,128)(2,1)S(1)} %pad_maximum_fusion), channel_id=1, source_target_pairs={{0,16},{16,0},{32,48},{48,32},{64,80},{80,64},{96,112},{112,96},{1... | collective-permute-start | bytes 1179656 | tf_op jit(solution)/shard_map/ppermute | solution.py:24
  32.3 12.6 %collective-permute-start.9 = (bf16[768,256]{1,0:T(8,128)(2,1)S(1)}, bf16[768,256]{1,0:T(8,128)(2,1)S(1)}, u32[]{:S(2)}, u32[]{:S(2)}) collective-permute-start(bf16[768,256]{1,0:T(8,128)(2,1)S(1)} %collective-permute-done.5), channel_id=1, source_target_pairs={{0,16},{16,0},{32,48},{48,32},{64,80},{80,64},{96,112},{112,96},{1... | collective-permute-start | bytes 1179656 | tf_op jit(solution)/shard_map/ppermute | solution.py:24
  39.1 5.8 %collective-permute-start.8 = (bf16[768,256]{1,0:T(8,128)(2,1)S(1)}, bf16[768,256]{1,0:T(8,128)(2,1)S(1)}, u32[]{:S(2)}, u32[]{:S(2)}) collective-permute-start(bf16[768,256]{1,0:T(8,128)(2,1)S(1)} %collective-permute-done.4), channel_id=1, source_target_pairs={{0,16},{16,0},{32,48},{48,32},{64,80},{80,64},{96,112},{112,96},{1... | collective-permute-start | bytes 1179656 | tf_op jit(solution)/shard_map/ppermute | solution.py:24
  41.1 3.9 %collective-permute-start.7 = (bf16[768,256]{1,0:T(8,128)(2,1)S(1)}, bf16[768,256]{1,0:T(8,128)(2,1)S(1)}, u32[]{:S(2)}, u32[]{:S(2)}) collective-permute-start(bf16[768,256]{1,0:T(8,128)(2,1)S(1)} %collective-permute-done.3), channel_id=1, source_target_pairs={{0,16},{16,0},{32,48},{48,32},{64,80},{80,64},{96,112},{112,96},{1... | collective-permute-start | bytes 1179656 | tf_op jit(solution)/shard_map/ppermute | solution.py:24
  44.9 2.2 %copy-start.1 = (bf16[1,1,256,64,128]{4,3,2,1,0:T(8,128)(2,1)S(1)}, bf16[1,1,256,64,128]{4,3,2,1,0:T(8,128)(2,1)}, u32[]{:S(2)}) copy-start(bf16[1,1,256,64,128]{4,3,2,1,0:T(8,128)(2,1)} %param.8) | copy-start | bytes 12582916

commit v2 on v1

--- a/solution.py
+++ b/solution.py
@@ -1,3 +1,5 @@
+import functools
+
 import jax
 import jax.numpy as jnp
 from jax import lax
@@ -24,12 +26,23 @@
     return lax.ppermute(value, "row", row_shift(dy, dx, dcore))
 
 
-def spmm_kernel(rows, cols, live, *refs):
-    parts, tiles_hbm, out, table, tiles, total, part_sem, tile_sem = refs[:8], *refs[8:]
-    part_tiles = table.shape[0] // len(parts)
+def z_groups(n_col):
+    return [[z * 2 + half for z in range(n_col // 2)] for half in range(2)]
+
+
+def spmm_kernel(lane_block, rows, cols, live, half, *refs):
+    n_parts = 8
+    parts, tiles_hbm = refs[:n_parts], refs[n_parts]
+    outs, (table, tiles, total, part_sem, tile_sem) = refs[n_parts + 1 : -5], refs[-5:]
+    part_tiles = table.shape[0] // n_parts
+    width = table.shape[2]
     pair_chunk = tiles.shape[0] // CHUNKS
     part_copies = [
-        pltpu.make_async_copy(part, table.at[pl.ds(i * part_tiles, part_tiles)], part_sem.at[i])
+        pltpu.make_async_copy(
+            part.at[:, :, pl.ds(lane_block * width, width)],
+            table.at[pl.ds(i * part_tiles, part_tiles)],
+            part_sem.at[i],
+        )
         for i, part in enumerate(parts)
     ]
     tile_copies = [
@@ -70,24 +83,56 @@
             return carry
 
         lax.fori_loop(0, jnp.clip(steps - chunk * chunk_steps, 0, chunk_steps), step, 0)
-    row_tiles = out.shape[0] // TILE
-    out[...] = total[:row_tiles].reshape(out.shape).astype(out.dtype)
+
+    row_tiles = total.shape[0] - 1
+    if len(outs) == 1:
+        outs[0][...] = total[:row_tiles].astype(outs[0].dtype)
+    else:
+        n_blocks = outs[0].shape[0]
+        block_tiles = outs[0].shape[1]
+        for z in range(n_blocks):
+            for out, side in zip(outs, (half[0], 1 - half[0])):
+                first = (2 * z + side) * block_tiles
+                out[z] = total[pl.ds(first, block_tiles)].astype(out.dtype)
+
+
+def spmm(lane_block, rows, cols, live, half, parts, tiles, row_tiles, outs):
+    width = parts[0].shape[2] // 2
+    scalar = pl.BlockSpec(memory_space=pltpu.SMEM)
+    anywhere = pl.BlockSpec(memory_space=pl.ANY)
+    flops = 2 * 2 * tiles.size * width
+    return pl.pallas_call(
+        functools.partial(spmm_kernel, lane_block),
+        out_shape=outs,
+        in_specs=[scalar] * 4 + [anywhere] * len(parts) + [pl.BlockSpec(memory_space=pltpu.HBM)],
+        out_specs=[pl.BlockSpec(memory_space=pltpu.VMEM)] * len(outs),
+        scratch_shapes=[
+            pltpu.VMEM((len(parts) * parts[0].shape[0], TILE, width), jnp.bfloat16),
+            pltpu.VMEM(tiles.shape, jnp.bfloat16),
+            pltpu.VMEM((row_tiles + 1, TILE, width), jnp.float32),
+            pltpu.SemaphoreType.DMA((len(parts),)),
+            pltpu.SemaphoreType.DMA((CHUNKS,)),
+        ],
+        compiler_params=pltpu.CompilerParams(vmem_limit_bytes=36 << 20),
+        cost_estimate=pl.CostEstimate(flops=flops, bytes_accessed=8 << 20, transcendentals=0),
+    )(rows, cols, live, half, *parts, tiles)
 
 
 def body(features, weight, tiles, tile_rows, tile_cols, counts):
     own, width = features.shape
     slots = tile_rows.shape[2]
     n_col = lax.axis_size("col")
+    n_z = n_col // 2
     row_tiles = n_col * own // TILE
     own_tiles = own // TILE
+    lanes = width // 2
     me = lax.axis_index("row")
     my_y, my_x, my_core = me // (X_CHIPS * CORES), me // CORES % X_CHIPS, me % CORES
+    my_half = lax.axis_index("col") % 2
+    other_half = [(c, c ^ 1) for c in range(n_col)]
 
     product = jnp.dot(features, weight, preferred_element_type=jnp.float32).astype(jnp.bfloat16)
-    column = jnp.concatenate([product] + [shift(product, k, 0, 0) for k in (1, 2, 3)], axis=0)
-    near = [column, shift(column, 0, 1, 0), shift(column, 0, 3, 0), shift(column, 0, 2, 0)]
-    far = [shift(v, 0, 0, 1) for v in near]
-    parts = [v.reshape(-1, TILE, width) for v in near + far]
+    pieces = [product] + [shift(product, k, 0, 0) for k in (1, 2, 3)]
 
     live = counts[0]
     rows = jnp.where(jnp.arange(slots, dtype=jnp.int32) < live, tile_rows[0, 0], row_tiles)
@@ -96,27 +141,39 @@
     back_y, back_x = (my_y - y) % Y_CHIPS, (my_x - x) % X_CHIPS
     place_x = jnp.where(back_x >= 2, 5 - back_x, back_x)
     cols = (((core + my_core) % 2 * X_CHIPS + place_x) * Y_CHIPS + back_y) * own_tiles + inner
+    *pieces, rows, cols = lax.optimization_barrier((*pieces, rows, cols))
 
-    scalar = pl.BlockSpec(memory_space=pltpu.SMEM)
-    hbm = pl.BlockSpec(memory_space=pl.ANY)
-    partial_rows = pl.pallas_call(
-        spmm_kernel,
-        out_shape=jax.ShapeDtypeStruct((row_tiles * TILE, width), jnp.bfloat16),
-        in_specs=[scalar] * 3 + [hbm] * 9,
-        out_specs=pl.BlockSpec(memory_space=pltpu.VMEM),
-        scratch_shapes=[
-            pltpu.VMEM((8 * parts[0].shape[0], TILE, width), jnp.bfloat16),
-            pltpu.VMEM(tiles.shape[2:], jnp.bfloat16),
-            pltpu.VMEM((row_tiles + 1, TILE, width), jnp.float32),
-            pltpu.SemaphoreType.DMA((8,)),
-            pltpu.SemaphoreType.DMA((CHUNKS,)),
-        ],
-        compiler_params=pltpu.CompilerParams(vmem_limit_bytes=32 << 20),
-    )(rows, cols, live, *parts, tiles[0, 0])
+    column = jnp.concatenate(pieces, axis=0)
+    near = [column, shift(column, 0, 1, 0), shift(column, 0, 3, 0), shift(column, 0, 2, 0)]
+    far = [shift(v, 0, 0, 1) for v in near]
+    parts = [v.reshape(-1, TILE, width) for v in near + far]
 
-    received = lax.all_to_all(partial_rows, "col", 0, 0, tiled=True)
-    received = received.reshape(n_col, own, width).astype(jnp.float32)
-    return jnp.maximum(jnp.sum(received, axis=0), 0.0).astype(jnp.bfloat16)
+    def call(lane_block, outs):
+        half = my_half.reshape(1).astype(jnp.int32)
+        return spmm(lane_block, rows, cols, live, half, parts, tiles[0, 0], row_tiles, outs)
+
+    kept = jax.ShapeDtypeStruct((n_z, own_tiles, TILE, lanes), jnp.float32)
+    sent = jax.ShapeDtypeStruct((n_z, own_tiles, TILE, lanes), jnp.bfloat16)
+    near_sum, far_sum = call(0, [kept, sent])
+    arrived = lax.ppermute(far_sum, "col", other_half)
+
+    whole = jax.ShapeDtypeStruct((row_tiles, TILE, lanes), jnp.bfloat16)
+    (second,) = call(1, [whole])
+    groups = z_groups(n_col)
+    second = lax.all_to_all(
+        second.reshape(n_z, 2, own, lanes), "col", 0, 0, axis_index_groups=groups, tiled=True
+    )
+    second = jnp.sum(second.astype(jnp.float32), axis=0)
+    keep = jnp.where(my_half == 0, second[0], second[1])
+    send = jnp.where(my_half == 0, second[1], second[0]).astype(jnp.bfloat16)
+    second = keep + lax.ppermute(send, "col", other_half).astype(jnp.float32)
+
+    first = (near_sum + arrived.astype(jnp.float32)).astype(jnp.bfloat16)
+    first = lax.all_to_all(
+        first.reshape(n_z, own, lanes), "col", 0, 0, axis_index_groups=groups, tiled=True
+    )
+    first = jnp.sum(first.astype(jnp.float32), axis=0)
+    return jnp.maximum(jnp.concatenate([first, second], axis=1), 0.0).astype(jnp.bfloat16)
 
 
 def solution(mesh):

time: 132 us -> 134 us (1.015)
  the two profiles are of different devices: /device:TPU:22 before, /device:TPU:17 now
where the time goes in v2:
time: 134 us; the launch traced here: 133 us
  starting transfers between devices  73.8 us (55%)
  waiting for transfers between devices  25.2 us (19%)
  Pallas kernels  21.7 us (16%)
  local copies, waits for them, and re-layouts  5.31 us (4%)
  other arithmetic  4.97 us (4%)
    ppermute x10, starting transfers between devices, shift(): return lax.ppermute(value, 'row', row_shift(dy, dx, dcore))  40.5 us
    pallas_call x2, Pallas kernels, spmm(): pl.pallas_call(functools.partial(spmm_kernel, lane_block), out_shape=outs...  21.7 us
    ppermute x1, waiting for transfers between devices, body(): arrived = lax.ppermute(far_sum, 'col', other_half)  15.3 us
    all_to_all x1, starting transfers between devices, body(): lax.all_to_all(first.reshape(n_z, own, lanes), 'col', 0, 0, axis_index_gr...  10.2 us
    all_to_all x1, starting transfers between devices, body(): lax.all_to_all(second.reshape(n_z, 2, own, lanes), 'col', 0, 0, axis_inde...  9.33 us
    all_to_all x1, waiting for transfers between devices, body(): lax.all_to_all(first.reshape(n_z, own, lanes), 'col', 0, 0, axis_index_gr...  8.64 us
    ppermute x1, starting transfers between devices, body(): arrived = lax.ppermute(far_sum, 'col', other_half)  8.62 us
    unnamed x9, local copies, waits for them, and re-layouts  5.3 us
  transfers between devices with their start and end apart: 14, of which 3 were waited for; matrix products, arithmetic and copies ran while one was open for 3% of the time, Pallas kernels for 8%

profile of v2, /device:TPU:17, one launch (start us, length us, event | category | flops | bytes accessed | tf_op | source)
XLA Modules:
  0.0 133.1 jit_solution(14228559059595834613)
XLA Ops:
  0.0 0.0 copy-start
  0.0 0.9 copy-done
  0.9 1.1 convolution_convert_fusion
  2.0 3.2 %collective-permute-start = (bf16[192,256]{1,0:T(8,128)(2,1)S(1)}, bf16[192,256]{1,0:T(8,128)(2,1)S(1)}, u32[]{:S(2)}, u32[]{:S(2)}) collective-permute-start(bf16[192,256]{1,0:T(8,128)(2,1)S(1)} %convolution_convert_fusion), channel_id=1, source_target_pairs={{0,128},{16,144},{32,160},{48,176},{64,192},{80,208},{96,224},{112... | collective-permute-start | bytes 294920 | tf_op jit(solution)/shard_map/ppermute | solution.py:26
  5.2 2.0 %collective-permute-start.1 = (bf16[192,256]{1,0:T(8,128)(2,1)S(1)}, bf16[192,256]{1,0:T(8,128)(2,1)S(1)}, u32[]{:S(2)}, u32[]{:S(2)}) collective-permute-start(bf16[192,256]{1,0:T(8,128)(2,1)S(1)} %convolution_convert_fusion), channel_id=1, source_target_pairs={{0,256},{16,272},{32,288},{48,304},{64,320},{80,336},{96,352},{112... | collective-permute-start | bytes 294920 | tf_op jit(solution)/shard_map/ppermute | solution.py:26
  7.2 3.0 %collective-permute-start.2 = (bf16[192,256]{1,0:T(8,128)(2,1)S(1)}, bf16[192,256]{1,0:T(8,128)(2,1)S(1)}, u32[]{:S(2)}, u32[]{:S(2)}) collective-permute-start(bf16[192,256]{1,0:T(8,128)(2,1)S(1)} %convolution_convert_fusion), channel_id=1, source_target_pairs={{0,384},{16,400},{32,416},{48,432},{64,448},{80,464},{96,480},{112... | collective-permute-start | bytes 294920 | tf_op jit(solution)/shard_map/ppermute | solution.py:26
  10.2 0.7 broadcast_divide_fusion
  10.9 0.7 compare_reduce_fusion
  12.3 0.7 fusion.9
  13.0 0.0 collective-permute-done
  13.1 0.0 collective-permute-done.1
  13.1 0.0 collective-permute-done.2
  13.1 3.3 %collective-permute-start.3 = (bf16[768,256]{1,0:T(8,128)(2,1)S(1)}, bf16[768,256]{1,0:T(8,128)(2,1)S(1)}, u32[]{:S(2)}, u32[]{:S(2)}) collective-permute-start(bf16[768,256]{1,0:T(8,128)(2,1)S(1)} %constant_dynamic-update-slice_fusion), channel_id=1, source_target_pairs={{0,32},{16,48},{32,64},{48,80},{64,96},{80,112},{96,0},{112,16},{1... | collective-permute-start | bytes 1179656 | tf_op jit(solution)/shard_map/ppermute | solution.py:26
  16.4 3.2 %collective-permute-start.4 = (bf16[768,256]{1,0:T(8,128)(2,1)S(1)}, bf16[768,256]{1,0:T(8,128)(2,1)S(1)}, u32[]{:S(2)}, u32[]{:S(2)}) collective-permute-start(bf16[768,256]{1,0:T(8,128)(2,1)S(1)} %constant_dynamic-update-slice_fusion), channel_id=1, source_target_pairs={{0,96},{16,112},{32,0},{48,16},{64,32},{80,48},{96,64},{112,80},{1... | collective-permute-start | bytes 1179656 | tf_op jit(solution)/shard_map/ppermute | solution.py:26
  19.7 3.6 %collective-permute-start.5 = (bf16[768,256]{1,0:T(8,128)(2,1)S(1)}, bf16[768,256]{1,0:T(8,128)(2,1)S(1)}, u32[]{:S(2)}, u32[]{:S(2)}) collective-permute-start(bf16[768,256]{1,0:T(8,128)(2,1)S(1)} %constant_dynamic-update-slice_fusion), channel_id=1, source_target_pairs={{0,64},{16,80},{32,96},{48,112},{64,0},{80,16},{96,32},{112,48},{1... | collective-permute-start | bytes 1179656 | tf_op jit(solution)/shard_map/ppermute | solution.py:26
  23.2 7.6 %collective-permute-start.6 = (bf16[768,256]{1,0:T(8,128)(2,1)S(1)}, bf16[768,256]{1,0:T(8,128)(2,1)S(1)}, u32[]{:S(2)}, u32[]{:S(2)}) collective-permute-start(bf16[768,256]{1,0:T(8,128)(2,1)S(1)} %constant_dynamic-update-slice_fusion), channel_id=1, source_target_pairs={{0,16},{16,0},{32,48},{48,32},{64,80},{80,64},{96,112},{112,96},{1... | collective-permute-start | bytes 1179656 | tf_op jit(solution)/shard_map/ppermute | solution.py:26
  30.9 0.0 collective-permute-done.3
  30.9 10.3 %collective-permute-start.7 = (bf16[768,256]{1,0:T(8,128)(2,1)S(1)}, bf16[768,256]{1,0:T(8,128)(2,1)S(1)}, u32[]{:S(2)}, u32[]{:S(2)}) collective-permute-start(bf16[768,256]{1,0:T(8,128)(2,1)S(1)} %collective-permute-done.3), channel_id=1, source_target_pairs={{0,16},{16,0},{32,48},{48,32},{64,80},{80,64},{96,112},{112,96},{1... | collective-permute-start | bytes 1179656 | tf_op jit(solution)/shard_map/ppermute | solution.py:26
  41.2 0.0 collective-permute-done.4
  41.2 1.9 %collective-permute-start.8 = (bf16[768,256]{1,0:T(8,128)(2,1)S(1)}, bf16[768,256]{1,0:T(8,128)(2,1)S(1)}, u32[]{:S(2)}, u32[]{:S(2)}) collective-permute-start(bf16[768,256]{1,0:T(8,128)(2,1)S(1)} %collective-permute-done.4), channel_id=1, source_target_pairs={{0,16},{16,0},{32,48},{48,32},{64,80},{80,64},{96,112},{112,96},{1... | collective-permute-start | bytes 1179656 | tf_op jit(solution)/shard_map/ppermute | solution.py:26
  43.1 0.0 collective-permute-done.5
  43.1 2.4 %collective-permute-start.9 = (bf16[768,256]{1,0:T(8,128)(2,1)S(1)}, bf16[768,256]{1,0:T(8,128)(2,1)S(1)}, u32[]{:S(2)}, u32[]{:S(2)}) collective-permute-start(bf16[768,256]{1,0:T(8,128)(2,1)S(1)} %collective-permute-done.5), channel_id=1, source_target_pairs={{0,16},{16,0},{32,48},{48,32},{64,80},{80,64},{96,112},{112,96},{1... | collective-permute-start | bytes 1179656 | tf_op jit(solution)/shard_map/ppermute | solution.py:26
  45.6 0.0 collective-permute-done.6
  45.6 0.0 collective-permute-done.7
  45.6 0.0 collective-permute-done.8
  45.6 1.3 collective-permute-done.9
  46.9 0.0 copy-start.1
  46.9 2.2 %copy-done.1 = bf16[1,1,256,64,128]{4,3,2,1,0:T(8,128)(2,1)S(1)} copy-done((bf16[1,1,256,64,128]{4,3,2,1,0:T(8,128)(2,1)S(1)}, bf16[1,1,256,64,128]{4,3,2,1,0:T(8,128)(2,1)}, u32[]{:S(2)}) %copy-start.1) | copy-done | bytes 4194328
  49.1 11.3 %shard_map.65 = bf16[48,64,128]{2,1,0:T(8,128)(2,1)} custom-call(s32[512]{0:T(512)S(1)} %get-tuple-element.13.rows, s32[512]{0:T(512)S(1)} %get-tuple-element.14.cols, s32[1]{0:T(128)} %bitcast.25.live, s32[1]{0:T(128)} %bitcast.5.half, bf16[12,64,256]{2,1,0:T(8,128)(2,1)S(1)} %bitcast.28, bf16[12,64,256]{2,1,0:T(8,128)(2,1)S(1)} %bitcast.30, ...), custom_call_target="tpu_custom_call" | custom-call | flops 1073741824 | bytes 8388608 | tf_op jit(solution)/shard_map/pallas_call | solution.py:104
  60.4 9.3 %all-to-all-start.1 = ((bf16[8,2,192,128]{3,2,1,0:T(8,128)(2,1)}), bf16[8,2,192,128]{3,2,1,0:T(8,128)(2,1)}, u32[]{:S(2)}, u32[]{:S(2)}) async-start(bf16[8,2,192,128]{3,2,1,0:T(8,128)(2,1)} %bitcast.16), calls=%async_computation.1 | async-start | bytes 1572864 | tf_op jit(solution)/shard_map/all_to_all | solution.py:163
  69.7 0.0 copy-start.2
  69.7 2.2 %copy-done.2 = bf16[1,1,256,64,128]{4,3,2,1,0:T(8,128)(2,1)S(1)} copy-done((bf16[1,1,256,64,128]{4,3,2,1,0:T(8,128)(2,1)S(1)}, bf16[1,1,256,64,128]{4,3,2,1,0:T(8,128)(2,1)}, u32[]{:S(2)}) %copy-start.2) | copy-done | bytes 4194328
  71.9 10.4 %shard_map.64 = (f32[8,3,64,128]{3,2,1,0:T(8,128)S(1)}, bf16[8,3,64,128]{3,2,1,0:T(8,128)(2,1)S(1)}) custom-call(s32[512]{0:T(512)S(1)} %get-tuple-element.13.rows, s32[512]{0:T(512)S(1)} %get-tuple-element.14.cols, s32[1]{0:T(128)} %bitcast.24.live, s32[1]{0:T(128)} %bitcast.5.half, bf16[12,64,256]{2,1,0:T(8,128)(2,1)S(1)} %bitcast.29, ...), custom_call_target="tpu_custom_call" | custom-call | flops 1073741824 | bytes 8388608 | tf_op jit(solution)/shard_map/pallas_call | solution.py:104
  82.3 8.6 %collective-permute-start.10 = (bf16[8,3,64,128]{3,2,1,0:T(8,128)(2,1)S(1)}, bf16[8,3,64,128]{3,2,1,0:T(8,128)(2,1)S(1)}, u32[]{:S(2)}, u32[]{:S(2)}) collective-permute-start(bf16[8,3,64,128]{3,2,1,0:T(8,128)(2,1)S(1)} %get-tuple-element.20), channel_id=1, source_target_pairs={{0,1},{1,0},{2,3},{3,2},{4,5},{5,4},{6,7},{7,6},{8,9},{9,8},{10,11... | collective-permute-start | bytes 1179656 | tf_op jit(solution)/shard_map/ppermute | solution.py:158
  91.0 15.3 %collective-permute-done.10 = bf16[8,3,64,128]{3,2,1,0:T(8,128)(2,1)S(1)} collective-permute-done((bf16[8,3,64,128]{3,2,1,0:T(8,128)(2,1)S(1)}, bf16[8,3,64,128]{3,2,1,0:T(8,128)(2,1)S(1)}, u32[]{:S(2)}, u32[]{:S(2)}) %collective-permute-start.10) | collective-permute-done | bytes 393248 | tf_op jit(solution)/shard_map/ppermute | solution.py:158
  106.2 0.8 add_convert_fusion
  107.1 0.0 all-to-all-done.1
  107.1 10.2 %all-to-all-start = ((bf16[8,192,128]{2,1,0:T(8,128)(2,1)}), bf16[8,192,128]{2,1,0:T(8,128)(2,1)S(1)}, u32[]{:S(2)}, u32[]{:S(2)}) async-start(bf16[8,192,128]{2,1,0:T(8,128)(2,1)} %bitcast.15), calls=%async_computation | async-start | bytes 786432 | tf_op jit(solution)/shard_map/all_to_all | solution.py:172
  117.3 1.3 convert_reduce_fusion
  118.6 5.2 %collective-permute-start.11 = (bf16[192,128]{1,0:T(8,128)(2,1)S(1)}, bf16[192,128]{1,0:T(8,128)(2,1)S(1)}, u32[]{:S(2)}, u32[]{:S(2)}) collective-permute-start(bf16[192,128]{1,0:T(8,128)(2,1)S(1)} %fusion.1), channel_id=1, source_target_pairs={{0,1},{1,0},{2,3},{3,2},{4,5},{5,4},{6,7},{7,6},{8,9},{9,8},{10,11... | collective-permute-start | bytes 147464 | tf_op jit(solution)/shard_map/ppermute | solution.py:169
  123.7 8.6 %all-to-all-done = bf16[8,192,128]{2,1,0:T(8,128)(2,1)S(1)} async-done(((bf16[8,192,128]{2,1,0:T(8,128)(2,1)}), bf16[8,192,128]{2,1,0:T(8,128)(2,1)S(1)}, u32[]{:S(2)}, u32[]{:S(2)}) %all-to-all-start) | async-done | bytes 393248 | tf_op jit(solution)/shard_map/all_to_all | solution.py:172
  132.4 0.1 convert_reduce_fusion.1
  132.4 0.0 collective-permute-done.11
  132.5 0.7 fusion
  (6 shorter events, 0.1 us)
Async XLA Ops:
  0.0 0.9 copy-start
  2.0 11.1 %collective-permute-start = (bf16[192,256]{1,0:T(8,128)(2,1)S(1)}, bf16[192,256]{1,0:T(8,128)(2,1)S(1)}, u32[]{:S(2)}, u32[]{:S(2)}) collective-permute-start(bf16[192,256]{1,0:T(8,128)(2,1)S(1)} %convolution_convert_fusion), channel_id=1, source_target_pairs={{0,128},{16,144},{32,160},{48,176},{64,192},{80,208},{96,224},{112... | collective-permute-start | bytes 294920 | tf_op jit(solution)/shard_map/ppermute | solution.py:26
  5.2 7.9 %collective-permute-start.1 = (bf16[192,256]{1,0:T(8,128)(2,1)S(1)}, bf16[192,256]{1,0:T(8,128)(2,1)S(1)}, u32[]{:S(2)}, u32[]{:S(2)}) collective-permute-start(bf16[192,256]{1,0:T(8,128)(2,1)S(1)} %convolution_convert_fusion), channel_id=1, source_target_pairs={{0,256},{16,272},{32,288},{48,304},{64,320},{80,336},{96,352},{112... | collective-permute-start | bytes 294920 | tf_op jit(solution)/shard_map/ppermute | solution.py:26
  7.2 5.9 %collective-permute-start.2 = (bf16[192,256]{1,0:T(8,128)(2,1)S(1)}, bf16[192,256]{1,0:T(8,128)(2,1)S(1)}, u32[]{:S(2)}, u32[]{:S(2)}) collective-permute-start(bf16[192,256]{1,0:T(8,128)(2,1)S(1)} %convolution_convert_fusion), channel_id=1, source_target_pairs={{0,384},{16,400},{32,416},{48,432},{64,448},{80,464},{96,480},{112... | collective-permute-start | bytes 294920 | tf_op jit(solution)/shard_map/ppermute | solution.py:26
  13.1 17.7 %collective-permute-start.3 = (bf16[768,256]{1,0:T(8,128)(2,1)S(1)}, bf16[768,256]{1,0:T(8,128)(2,1)S(1)}, u32[]{:S(2)}, u32[]{:S(2)}) collective-permute-start(bf16[768,256]{1,0:T(8,128)(2,1)S(1)} %constant_dynamic-update-slice_fusion), channel_id=1, source_target_pairs={{0,32},{16,48},{32,64},{48,80},{64,96},{80,112},{96,0},{112,16},{1... | collective-permute-start | bytes 1179656 | tf_op jit(solution)/shard_map/ppermute | solution.py:26
  16.4 24.8 %collective-permute-start.4 = (bf16[768,256]{1,0:T(8,128)(2,1)S(1)}, bf16[768,256]{1,0:T(8,128)(2,1)S(1)}, u32[]{:S(2)}, u32[]{:S(2)}) collective-permute-start(bf16[768,256]{1,0:T(8,128)(2,1)S(1)} %constant_dynamic-update-slice_fusion), channel_id=1, source_target_pairs={{0,96},{16,112},{32,0},{48,16},{64,32},{80,48},{96,64},{112,80},{1... | collective-permute-start | bytes 1179656 | tf_op jit(solution)/shard_map/ppermute | solution.py:26
  19.7 23.5 %collective-permute-start.5 = (bf16[768,256]{1,0:T(8,128)(2,1)S(1)}, bf16[768,256]{1,0:T(8,128)(2,1)S(1)}, u32[]{:S(2)}, u32[]{:S(2)}) collective-permute-start(bf16[768,256]{1,0:T(8,128)(2,1)S(1)} %constant_dynamic-update-slice_fusion), channel_id=1, source_target_pairs={{0,64},{16,80},{32,96},{48,112},{64,0},{80,16},{96,32},{112,48},{1... | collective-permute-start | bytes 1179656 | tf_op jit(solution)/shard_map/ppermute | solution.py:26
  23.2 22.3 %collective-permute-start.6 = (bf16[768,256]{1,0:T(8,128)(2,1)S(1)}, bf16[768,256]{1,0:T(8,128)(2,1)S(1)}, u32[]{:S(2)}, u32[]{:S(2)}) collective-permute-start(bf16[768,256]{1,0:T(8,128)(2,1)S(1)} %constant_dynamic-update-slice_fusion), channel_id=1, source_target_pairs={{0,16},{16,0},{32,48},{48,32},{64,80},{80,64},{96,112},{112,96},{1... | collective-permute-start | bytes 1179656 | tf_op jit(solution)/shard_map/ppermute | solution.py:26
  30.9 14.7 %collective-permute-start.7 = (bf16[768,256]{1,0:T(8,128)(2,1)S(1)}, bf16[768,256]{1,0:T(8,128)(2,1)S(1)}, u32[]{:S(2)}, u32[]{:S(2)}) collective-permute-start(bf16[768,256]{1,0:T(8,128)(2,1)S(1)} %collective-permute-done.3), channel_id=1, source_target_pairs={{0,16},{16,0},{32,48},{48,32},{64,80},{80,64},{96,112},{112,96},{1... | collective-permute-start | bytes 1179656 | tf_op jit(solution)/shard_map/ppermute | solution.py:26
  41.2 4.4 %collective-permute-start.8 = (bf16[768,256]{1,0:T(8,128)(2,1)S(1)}, bf16[768,256]{1,0:T(8,128)(2,1)S(1)}, u32[]{:S(2)}, u32[]{:S(2)}) collective-permute-start(bf16[768,256]{1,0:T(8,128)(2,1)S(1)} %collective-permute-done.4), channel_id=1, source_target_pairs={{0,16},{16,0},{32,48},{48,32},{64,80},{80,64},{96,112},{112,96},{1... | collective-permute-start | bytes 1179656 | tf_op jit(solution)/shard_map/ppermute | solution.py:26
  43.1 3.7 %collective-permute-start.9 = (bf16[768,256]{1,0:T(8,128)(2,1)S(1)}, bf16[768,256]{1,0:T(8,128)(2,1)S(1)}, u32[]{:S(2)}, u32[]{:S(2)}) collective-permute-start(bf16[768,256]{1,0:T(8,128)(2,1)S(1)} %collective-permute-done.5), channel_id=1, source_target_pairs={{0,16},{16,0},{32,48},{48,32},{64,80},{80,64},{96,112},{112,96},{1... | collective-permute-start | bytes 1179656 | tf_op jit(solution)/shard_map/ppermute | solution.py:26
  46.9 2.2 %copy-start.1 = (bf16[1,1,256,64,128]{4,3,2,1,0:T(8,128)(2,1)S(1)}, bf16[1,1,256,64,128]{4,3,2,1,0:T(8,128)(2,1)}, u32[]{:S(2)}) copy-start(bf16[1,1,256,64,128]{4,3,2,1,0:T(8,128)(2,1)} %param.8) | copy-start | bytes 12582916
  60.4 46.7 %all-to-all-start.1 = ((bf16[8,2,192,128]{3,2,1,0:T(8,128)(2,1)}), bf16[8,2,192,128]{3,2,1,0:T(8,128)(2,1)}, u32[]{:S(2)}, u32[]{:S(2)}) async-start(bf16[8,2,192,128]{3,2,1,0:T(8,128)(2,1)} %bitcast.16), calls=%async_computation.1 | async-start | bytes 1572864 | tf_op jit(solution)/shard_map/all_to_all | solution.py:163
  69.7 2.2 %copy-start.2 = (bf16[1,1,256,64,128]{4,3,2,1,0:T(8,128)(2,1)S(1)}, bf16[1,1,256,64,128]{4,3,2,1,0:T(8,128)(2,1)}, u32[]{:S(2)}) copy-start(bf16[1,1,256,64,128]{4,3,2,1,0:T(8,128)(2,1)} %param.8) | copy-start | bytes 12582916
  82.3 23.9 %collective-permute-start.10 = (bf16[8,3,64,128]{3,2,1,0:T(8,128)(2,1)S(1)}, bf16[8,3,64,128]{3,2,1,0:T(8,128)(2,1)S(1)}, u32[]{:S(2)}, u32[]{:S(2)}) collective-permute-start(bf16[8,3,64,128]{3,2,1,0:T(8,128)(2,1)S(1)} %get-tuple-element.20), channel_id=1, source_target_pairs={{0,1},{1,0},{2,3},{3,2},{4,5},{5,4},{6,7},{7,6},{8,9},{9,8},{10,11... | collective-permute-start | bytes 1179656 | tf_op jit(solution)/shard_map/ppermute | solution.py:158
  107.1 25.3 %all-to-all-start = ((bf16[8,192,128]{2,1,0:T(8,128)(2,1)}), bf16[8,192,128]{2,1,0:T(8,128)(2,1)S(1)}, u32[]{:S(2)}, u32[]{:S(2)}) async-start(bf16[8,192,128]{2,1,0:T(8,128)(2,1)} %bitcast.15), calls=%async_computation | async-start | bytes 786432 | tf_op jit(solution)/shard_map/all_to_all | solution.py:172
  118.6 13.9 %collective-permute-start.11 = (bf16[192,128]{1,0:T(8,128)(2,1)S(1)}, bf16[192,128]{1,0:T(8,128)(2,1)S(1)}, u32[]{:S(2)}, u32[]{:S(2)}) collective-permute-start(bf16[192,128]{1,0:T(8,128)(2,1)S(1)} %fusion.1), channel_id=1, source_target_pairs={{0,1},{1,0},{2,3},{3,2},{4,5},{5,4},{6,7},{7,6},{8,9},{9,8},{10,11... | collective-permute-start | bytes 147464 | tf_op jit(solution)/shard_map/ppermute | solution.py:169

commit v3 on v0

v3 whole, which is shorter than its diff:
```python
import jax
import jax.numpy as jnp
from jax import lax
from jax.experimental import pallas as pl
from jax.experimental.pallas import tpu as pltpu
from jax.sharding import PartitionSpec as P

TILE = 64
Y_CHIPS, X_CHIPS, CORES = 4, 4, 2
GROUP = 4
UNROLL = 8
CHUNKS = 4


def shift(value, dy, dx):
    pairs = []
    for source in range(Y_CHIPS * X_CHIPS * CORES):
        y, x, core = source // (X_CHIPS * CORES), source // CORES % X_CHIPS, source % CORES
        y, x = (y + dy) % Y_CHIPS, (x + dx) % X_CHIPS
        pairs.append((source, (y * X_CHIPS + x) * CORES + core))
    return lax.ppermute(value, "row", pairs)


def both_cores(value):
    groups = [[2 * chip, 2 * chip + 1] for chip in range(Y_CHIPS * X_CHIPS)]
    return lax.all_gather(value, "row", axis_index_groups=groups, axis=0, tiled=True)


def count(mask, axis):
    return jnp.sum(mask.astype(jnp.int32), axis=axis)


def plan(rows, cols, live, row_tiles):
    slots = rows.shape[0]
    groups = (slots + row_tiles) // 2
    groups = (groups + UNROLL - 1) // UNROLL * UNROLL
    slot = jnp.arange(slots, dtype=jnp.int32)
    odd = slot % 2
    row = jnp.where(slot < live, rows, row_tiles)
    key = row * 2 + odd
    rank = count((key[None, :] == key[:, None]) & (slot[None, :] < slot[:, None]), 1)
    row_id = jnp.arange(row_tiles, dtype=jnp.int32)
    evens = count(key[None, :] == 2 * row_id[:, None], 1)
    odds = count(key[None, :] == 2 * row_id[:, None] + 1, 1)
    held = (jnp.maximum(evens, odds) + 1) // 2
    ends = jnp.sum(jnp.where(row_id[None, :] <= row_id[:, None], held[None, :], 0), axis=1)
    base = jnp.sum(jnp.where(row_id[None, :] < row[:, None], held[None, :], 0), axis=1)
    place = jnp.where(slot < live, base * GROUP + rank * 2 + odd, groups * GROUP)
    spot = jnp.arange(groups * GROUP, dtype=jnp.int32)
    found = jnp.where(place[None, :] == spot[:, None], slot[None, :] * 128 + cols[None, :], -1)
    found = jnp.max(found, axis=1)
    block = jnp.where(found < 0, slots // 2, found // 256)
    column = jnp.where(found < 0, 0, found % 128)
    group = jnp.arange(groups, dtype=jnp.int32)
    group_row = count(ends[None, :] <= group[:, None], 1)
    return block, column, group_row, ends[row_tiles - 1 :]


def spmm_kernel(block, column, group_row, used, *refs):
    parts, tiles_hbm, out, table, tiles, total, sems = refs[:-6], *refs[-6:]
    pairs = tiles_hbm.shape[0]
    chunk = pairs // CHUNKS
    copies = [
        pltpu.make_async_copy(
            tiles_hbm.at[pl.ds(i * chunk, chunk)], tiles.at[pl.ds(i * chunk, chunk)], sems.at[i]
        )
        for i in range(CHUNKS)
    ]
    for copy in copies:
        copy.start()
    tiles[pairs] = jnp.zeros(tiles.shape[1:], tiles.dtype)
    total[...] = jnp.zeros_like(total)
    part_tiles = table.shape[0] // len(parts)
    for i, part in enumerate(parts):
        table[pl.ds(i * part_tiles, part_tiles)] = part[...]
    left = lax.broadcasted_iota(jnp.int32, (TILE, 2 * TILE), 1) < TILE
    for copy in copies:
        copy.wait()

    def step(i, carry):
        terms = []
        for j in range(UNROLL):
            spots = [(i * UNROLL + j) * GROUP + t for t in range(GROUP)]
            lhs = [
                jnp.where(left, tiles[block[spots[t]]], tiles[block[spots[t + 1]]])
                for t in range(0, GROUP, 2)
            ]
            rhs = [table[column[spot]] for spot in spots]
            terms.append(
                jnp.dot(
                    jnp.concatenate(lhs, axis=1),
                    jnp.concatenate(rhs, axis=0),
                    preferred_element_type=jnp.float32,
                )
            )
        for j in range(UNROLL):
            total[group_row[i * UNROLL + j]] += terms[j]
        return carry

    lax.fori_loop(0, (used[0] + UNROLL - 1) // UNROLL, step, 0)
    row_tiles = out.shape[0] // TILE
    out[...] = total[:row_tiles].reshape(out.shape).astype(out.dtype)


def spmm(block, column, group_row, used, parts, tiles, row_tiles):
    width = parts[0].shape[2]
    scalar = pl.BlockSpec(memory_space=pltpu.SMEM)
    vmem = pl.BlockSpec(memory_space=pltpu.VMEM)
    return pl.pallas_call(
        spmm_kernel,
        out_shape=jax.ShapeDtypeStruct((row_tiles * TILE, width), jnp.bfloat16),
        in_specs=[scalar] * 4 + [vmem] * len(parts) + [pl.BlockSpec(memory_space=pl.ANY)],
        out_specs=vmem,
        scratch_shapes=[
            pltpu.VMEM((len(parts) * parts[0].shape[0], TILE, width), jnp.bfloat16),
            pltpu.VMEM((tiles.shape[0] + 1, *tiles.shape[1:]), jnp.bfloat16),
            pltpu.VMEM((row_tiles + 1, TILE, width), jnp.float32),
            pltpu.SemaphoreType.DMA((CHUNKS,)),
        ],
        compiler_params=pltpu.CompilerParams(vmem_limit_bytes=VMEM_LIMIT),
    )(block, column, group_row, used, *parts, tiles)


VMEM_LIMIT = 48 << 20


def body(features, weight, tiles, tile_rows, tile_cols, counts):
    own, width = features.shape
    n_col = lax.axis_size("col")
    row_tiles = n_col * own // TILE
    own_tiles = own // TILE
    me = lax.axis_index("row")
    my_y, my_x = me // (X_CHIPS * CORES), me // CORES % X_CHIPS

    product = jnp.dot(features, weight, preferred_element_type=jnp.float32).astype(jnp.bfloat16)
    pieces = [product] + [shift(product, k, 0) for k in (1, 2, 3)]

    owner, inner = tile_cols[0, 0] // own_tiles, tile_cols[0, 0] % own_tiles
    y, x, core = owner // (X_CHIPS * CORES), owner // CORES % X_CHIPS, owner % CORES
    back_y, back_x = (my_y - y) % Y_CHIPS, (my_x - x) % X_CHIPS
    place_x = jnp.where(back_x >= 2, 5 - back_x, back_x)
    cols = ((place_x * CORES + core) * Y_CHIPS + back_y) * own_tiles + inner
    block, column, group_row, used = plan(tile_rows[0, 0], cols, counts[0, 0], row_tiles)
    *pieces, block, column, group_row, used = lax.optimization_barrier(
        (*pieces, block, column, group_row, used)
    )

    line = jnp.concatenate(pieces, axis=0)
    near = [line, shift(line, 0, 1), shift(line, 0, 3), shift(line, 0, 2)]
    parts = [both_cores(v).reshape(-1, TILE, width) for v in near]
    partial_rows = spmm(block, column, group_row, used, parts, tiles[0, 0], row_tiles)

    received = lax.all_to_all(partial_rows, "col", 0, 0, tiled=True)
    received = received.reshape(n_col, own, width).astype(jnp.float32)
    return jnp.maximum(jnp.sum(received, axis=0), 0.0).astype(jnp.bfloat16)


def solution(mesh):
    return jax.shard_map(
        body,
        mesh=mesh,
        in_specs=(
            P(("row", "col"), None),
            P(),
            P("row", "col", None, None, None),
            P("row", "col", None),
            P("row", "col", None),
            P("row", "col"),
        ),
        out_specs=P(("row", "col"), None),
        check_vma=False,
    )
```

time: 516 us -> 121 us (0.23)
  the two profiles are of different devices: /device:TPU:8 before, /device:TPU:20 now
where the time goes in v3:
time: 121 us
  blocking collectives  79.4 us (66%)
  starting transfers between devices  21.3 us (18%)
  Pallas kernels  6.82 us (6%)
  waiting for transfers between devices  5.43 us (4%)
  other arithmetic  4.16 us (3%)
  local copies, waits for them, and re-layouts  1.61 us (1%)
    all_to_all x1, blocking collectives, body(): received = lax.all_to_all(partial_rows, 'col', 0, 0, tiled=True)  70 us
    ppermute x6, starting transfers between devices, shift(): return lax.ppermute(value, 'row', pairs)  21.3 us
    all_gather x4, blocking collectives, both_cores(): lax.all_gather(value, 'row', axis_index_groups=groups, axis=0, tiled=True)  9.44 us
    pallas_call x1, Pallas kernels, spmm(): pl.pallas_call(spmm_kernel, out_shape=jax.ShapeDtypeStruct((row_tiles * T...  6.82 us
    ppermute x6, waiting for transfers between devices, shift(): return lax.ppermute(value, 'row', pairs)  5.43 us
  transfers between devices with their start and end apart: 6, of which 3 were waited for; matrix products, arithmetic and copies ran while one was open for 3% of the time, Pallas kernels for 0%

profile of v3, /device:TPU:20, one launch (start us, length us, event | category | flops | bytes accessed | tf_op | source)
XLA Modules:
  0.0 120.7 jit_solution(9896933243746394071)
XLA Ops:
  0.0 0.0 copy-start
  0.0 0.9 copy-done
  0.9 1.1 convolution_convert_fusion
  2.0 2.4 %collective-permute-start.2 = (bf16[192,256]{1,0:T(8,128)(2,1)S(1)}, bf16[192,256]{1,0:T(8,128)(2,1)S(1)}, u32[]{:S(2)}, u32[]{:S(2)}) collective-permute-start(bf16[192,256]{1,0:T(8,128)(2,1)S(1)} %convolution_convert_fusion), channel_id=1, source_target_pairs={{0,384},{16,400},{32,416},{48,432},{64,448},{80,464},{96,480},{112... | collective-permute-start | bytes 294920 | tf_op jit(solution)/shard_map/ppermute | solution.py:21
  4.3 5.4 %collective-permute-start.1 = (bf16[192,256]{1,0:T(8,128)(2,1)S(1)}, bf16[192,256]{1,0:T(8,128)(2,1)S(1)}, u32[]{:S(2)}, u32[]{:S(2)}) collective-permute-start(bf16[192,256]{1,0:T(8,128)(2,1)S(1)} %convolution_convert_fusion), channel_id=1, source_target_pairs={{0,256},{16,272},{32,288},{48,304},{64,320},{80,336},{96,352},{112... | collective-permute-start | bytes 294920 | tf_op jit(solution)/shard_map/ppermute | solution.py:21
  9.7 1.9 %collective-permute-start = (bf16[192,256]{1,0:T(8,128)(2,1)S(1)}, bf16[192,256]{1,0:T(8,128)(2,1)S(1)}, u32[]{:S(2)}, u32[]{:S(2)}) collective-permute-start(bf16[192,256]{1,0:T(8,128)(2,1)S(1)} %convolution_convert_fusion), channel_id=1, source_target_pairs={{0,128},{16,144},{32,160},{48,176},{64,192},{80,208},{96,224},{112... | collective-permute-start | bytes 294920 | tf_op jit(solution)/shard_map/ppermute | solution.py:21
  11.7 0.7 compare_reduce_fusion
  12.4 0.7 broadcast_divide_fusion
  13.8 0.7 fusion.21
  14.5 0.2 convert_reduce_fusion.1
  14.7 0.2 convert_reduce_fusion.2
  14.9 0.1 select_reduce_fusion.2
  15.0 0.1 select_reduce_fusion.1
  15.1 0.7 slice.3.used
  15.9 0.4 select_reduce_fusion
  16.3 0.1 convert_reduce_fusion.4.group_row
  16.4 0.0 collective-permute-done.2
  16.4 0.0 collective-permute-done.1
  16.4 0.4 collective-permute-done
  16.8 5.8 %collective-permute-start.5 = (bf16[768,256]{1,0:T(8,128)(2,1)S(1)}, bf16[768,256]{1,0:T(8,128)(2,1)S(1)}, u32[]{:S(2)}, u32[]{:S(2)}) collective-permute-start(bf16[768,256]{1,0:T(8,128)(2,1)S(1)} %constant_dynamic-update-slice_fusion), channel_id=1, source_target_pairs={{0,64},{16,80},{32,96},{48,112},{64,0},{80,16},{96,32},{112,48},{1... | collective-permute-start | bytes 1179656 | tf_op jit(solution)/shard_map/ppermute | solution.py:21
  22.7 1.9 %collective-permute-start.4 = (bf16[768,256]{1,0:T(8,128)(2,1)S(1)}, bf16[768,256]{1,0:T(8,128)(2,1)S(1)}, u32[]{:S(2)}, u32[]{:S(2)}) collective-permute-start(bf16[768,256]{1,0:T(8,128)(2,1)S(1)} %constant_dynamic-update-slice_fusion), channel_id=1, source_target_pairs={{0,96},{16,112},{32,0},{48,16},{64,32},{80,48},{96,64},{112,80},{1... | collective-permute-start | bytes 1179656 | tf_op jit(solution)/shard_map/ppermute | solution.py:21
  24.6 3.9 %collective-permute-start.3 = (bf16[768,256]{1,0:T(8,128)(2,1)S(1)}, bf16[768,256]{1,0:T(8,128)(2,1)S(1)}, u32[]{:S(2)}, u32[]{:S(2)}) collective-permute-start(bf16[768,256]{1,0:T(8,128)(2,1)S(1)} %constant_dynamic-update-slice_fusion), channel_id=1, source_target_pairs={{0,32},{16,48},{32,64},{48,80},{64,96},{80,112},{96,0},{112,16},{1... | collective-permute-start | bytes 1179656 | tf_op jit(solution)/shard_map/ppermute | solution.py:21
  28.5 2.4 %all_gather.12 = bf16[1536,256]{1,0:T(8,128)(2,1)S(1)} all-gather(bf16[768,256]{1,0:T(8,128)(2,1)S(1)} %constant_dynamic-update-slice_fusion), channel_id=1, replica_groups={{0,16},{32,48},{64,80},{96,112},{128,144},{160,176},{192,208},{224,240}..., dimensions={0}, use_global_device_ids=true | all-gather | bytes 1179648 | tf_op jit(solution)/shard_map/all_gather | solution.py:26
  30.9 1.8 %collective-permute-done.5 = bf16[768,256]{1,0:T(8,128)(2,1)S(1)} collective-permute-done((bf16[768,256]{1,0:T(8,128)(2,1)S(1)}, bf16[768,256]{1,0:T(8,128)(2,1)S(1)}, u32[]{:S(2)}, u32[]{:S(2)}) %collective-permute-start.5) | collective-permute-done | bytes 393248 | tf_op jit(solution)/shard_map/ppermute | solution.py:21
  32.7 2.4 %all_gather.15 = bf16[1536,256]{1,0:T(8,128)(2,1)S(1)} all-gather(bf16[768,256]{1,0:T(8,128)(2,1)S(1)} %collective-permute-done.5), channel_id=1, replica_groups={{0,16},{32,48},{64,80},{96,112},{128,144},{160,176},{192,208},{224,240}..., dimensions={0}, use_global_device_ids=true | all-gather | bytes 1179648 | tf_op jit(solution)/shard_map/all_gather | solution.py:26
  35.1 3.2 %collective-permute-done.4 = bf16[768,256]{1,0:T(8,128)(2,1)S(1)} collective-permute-done((bf16[768,256]{1,0:T(8,128)(2,1)S(1)}, bf16[768,256]{1,0:T(8,128)(2,1)S(1)}, u32[]{:S(2)}, u32[]{:S(2)}) %collective-permute-start.4) | collective-permute-done | bytes 393248 | tf_op jit(solution)/shard_map/ppermute | solution.py:21
  38.3 2.4 %all_gather.14 = bf16[1536,256]{1,0:T(8,128)(2,1)S(1)} all-gather(bf16[768,256]{1,0:T(8,128)(2,1)S(1)} %collective-permute-done.4), channel_id=1, replica_groups={{0,16},{32,48},{64,80},{96,112},{128,144},{160,176},{192,208},{224,240}..., dimensions={0}, use_global_device_ids=true | all-gather | bytes 1179648 | tf_op jit(solution)/shard_map/all_gather | solution.py:26
  40.6 0.0 collective-permute-done.3
  40.6 2.4 %all_gather.13 = bf16[1536,256]{1,0:T(8,128)(2,1)S(1)} all-gather(bf16[768,256]{1,0:T(8,128)(2,1)S(1)} %collective-permute-done.3), channel_id=1, replica_groups={{0,16},{32,48},{64,80},{96,112},{128,144},{160,176},{192,208},{224,240}..., dimensions={0}, use_global_device_ids=true | all-gather | bytes 1179648 | tf_op jit(solution)/shard_map/all_gather | solution.py:26
  43.0 6.8 %shard_map.64 = bf16[3072,256]{1,0:T(8,128)(2,1)S(1)} custom-call(s32[1120]{0:T(1024)S(1)} %get-tuple-element.13.block, s32[1120]{0:T(1024)S(1)} %get-tuple-element.14.column, s32[280]{0:T(512)S(1)} %convert_reduce_fusion.4.group_row, s32[1]{0:T(128)} %slice.3.used, bf16[24,64,256]{2,1,0:T(8,128)(2,1)S(1)} %bitcast.15, bf16[24,64,256]{2,1,0:T(8,128)(2,1)S(1)} %bitcast.18, ...), custom_call_target="tpu_custom_call" | custom-call | tf_op jit(solution)/shard_map/pallas_call | solution.py:109
  49.8 70.0 %all_to_all.9 = bf16[16,192,256]{2,1,0:T(8,128)(2,1)S(1)} all-to-all(bf16[16,192,256]{2,1,0:T(8,128)(2,1)S(1)} %bitcast.14), channel_id=1, replica_groups=mesh['row'=32,'col'=16] {'col'}, dimensions={0} | all-to-all | bytes 3145728 | tf_op jit(solution)/shard_map/all_to_all | solution.py:153
  119.8 0.2 convert_reduce_fusion
  120.0 0.7 maximum_convert_fusion
  (9 shorter events, 0.1 us)
Async XLA Ops:
  0.0 0.9 copy-start
  2.0 14.4 %collective-permute-start.2 = (bf16[192,256]{1,0:T(8,128)(2,1)S(1)}, bf16[192,256]{1,0:T(8,128)(2,1)S(1)}, u32[]{:S(2)}, u32[]{:S(2)}) collective-permute-start(bf16[192,256]{1,0:T(8,128)(2,1)S(1)} %convolution_convert_fusion), channel_id=1, source_target_pairs={{0,384},{16,400},{32,416},{48,432},{64,448},{80,464},{96,480},{112... | collective-permute-start | bytes 294920 | tf_op jit(solution)/shard_map/ppermute | solution.py:21
  4.3 12.0 %collective-permute-start.1 = (bf16[192,256]{1,0:T(8,128)(2,1)S(1)}, bf16[192,256]{1,0:T(8,128)(2,1)S(1)}, u32[]{:S(2)}, u32[]{:S(2)}) collective-permute-start(bf16[192,256]{1,0:T(8,128)(2,1)S(1)} %convolution_convert_fusion), channel_id=1, source_target_pairs={{0,256},{16,272},{32,288},{48,304},{64,320},{80,336},{96,352},{112... | collective-permute-start | bytes 294920 | tf_op jit(solution)/shard_map/ppermute | solution.py:21
  9.7 7.0 %collective-permute-start = (bf16[192,256]{1,0:T(8,128)(2,1)S(1)}, bf16[192,256]{1,0:T(8,128)(2,1)S(1)}, u32[]{:S(2)}, u32[]{:S(2)}) collective-permute-start(bf16[192,256]{1,0:T(8,128)(2,1)S(1)} %convolution_convert_fusion), channel_id=1, source_target_pairs={{0,128},{16,144},{32,160},{48,176},{64,192},{80,208},{96,224},{112... | collective-permute-start | bytes 294920 | tf_op jit(solution)/shard_map/ppermute | solution.py:21
  16.8 15.9 %collective-permute-start.5 = (bf16[768,256]{1,0:T(8,128)(2,1)S(1)}, bf16[768,256]{1,0:T(8,128)(2,1)S(1)}, u32[]{:S(2)}, u32[]{:S(2)}) collective-permute-start(bf16[768,256]{1,0:T(8,128)(2,1)S(1)} %constant_dynamic-update-slice_fusion), channel_id=1, source_target_pairs={{0,64},{16,80},{32,96},{48,112},{64,0},{80,16},{96,32},{112,48},{1... | collective-permute-start | bytes 1179656 | tf_op jit(solution)/shard_map/ppermute | solution.py:21
  22.7 15.6 %collective-permute-start.4 = (bf16[768,256]{1,0:T(8,128)(2,1)S(1)}, bf16[768,256]{1,0:T(8,128)(2,1)S(1)}, u32[]{:S(2)}, u32[]{:S(2)}) collective-permute-start(bf16[768,256]{1,0:T(8,128)(2,1)S(1)} %constant_dynamic-update-slice_fusion), channel_id=1, source_target_pairs={{0,96},{16,112},{32,0},{48,16},{64,32},{80,48},{96,64},{112,80},{1... | collective-permute-start | bytes 1179656 | tf_op jit(solution)/shard_map/ppermute | solution.py:21
  24.6 16.1 %collective-permute-start.3 = (bf16[768,256]{1,0:T(8,128)(2,1)S(1)}, bf16[768,256]{1,0:T(8,128)(2,1)S(1)}, u32[]{:S(2)}, u32[]{:S(2)}) collective-permute-start(bf16[768,256]{1,0:T(8,128)(2,1)S(1)} %constant_dynamic-update-slice_fusion), channel_id=1, source_target_pairs={{0,32},{16,48},{32,64},{48,80},{64,96},{80,112},{96,0},{112,16},{1... | collective-permute-start | bytes 1179656 | tf_op jit(solution)/shard_map/ppermute | solution.py:21

commit v4 on v3

v4 whole, which is shorter than its diff:
```python
import functools

import jax
import jax.numpy as jnp
from jax import lax
from jax.experimental import pallas as pl
from jax.experimental.pallas import tpu as pltpu
from jax.sharding import PartitionSpec as P

TILE = 64
Y_CHIPS, X_CHIPS, CORES = 4, 4, 2
GROUP = 4
UNROLL = 8
CHUNKS = 4


def shift(value, dy, dx):
    pairs = []
    for source in range(Y_CHIPS * X_CHIPS * CORES):
        y, x, core = source // (X_CHIPS * CORES), source // CORES % X_CHIPS, source % CORES
        y, x = (y + dy) % Y_CHIPS, (x + dx) % X_CHIPS
        pairs.append((source, (y * X_CHIPS + x) * CORES + core))
    return lax.ppermute(value, "row", pairs)


def both_cores(value):
    groups = [[2 * chip, 2 * chip + 1] for chip in range(Y_CHIPS * X_CHIPS)]
    return lax.all_gather(value, "row", axis_index_groups=groups, axis=0, tiled=True)


def count(mask, axis):
    return jnp.sum(mask.astype(jnp.int32), axis=axis)


def place_slots(rows, late, live, row_tiles):
    keys = 2 * row_tiles
    slot = jnp.arange(rows.shape[0], dtype=jnp.int32)
    odd = slot % 2
    key = jnp.where(slot < live, late * row_tiles + rows, keys)
    full_key = key * 2 + odd
    rank = count((full_key[None, :] == full_key[:, None]) & (slot[None, :] < slot[:, None]), 1)
    key_id = jnp.arange(keys, dtype=jnp.int32)
    evens = count(full_key[None, :] == 2 * key_id[:, None], 1)
    odds = count(full_key[None, :] == 2 * key_id[:, None] + 1, 1)
    held = (jnp.maximum(evens, odds) + 1) // 2
    early = jnp.sum(jnp.where(key_id < row_tiles, held, 0))
    early_steps = (early + UNROLL - 1) // UNROLL
    gap = early_steps * UNROLL - early
    skip = jnp.where(key_id < row_tiles, 0, gap)
    ends = jnp.sum(jnp.where(key_id[None, :] <= key_id[:, None], held[None, :], 0), axis=1) + skip
    base = jnp.sum(jnp.where(key_id[None, :] < key[:, None], held[None, :], 0), axis=1)
    base = base + jnp.where(key < row_tiles, 0, gap)
    place = jnp.where(slot < live, base * GROUP + rank * 2 + odd, -1)
    return place, ends, jnp.stack([early_steps, (jnp.max(ends) + UNROLL - 1) // UNROLL])


def fill_groups(place, ends, cols, row_tiles):
    slots = place.shape[0]
    groups = (slots + ends.shape[0]) // 2 + UNROLL - 1
    groups = (groups + UNROLL - 1) // UNROLL * UNROLL
    slot = jnp.arange(slots, dtype=jnp.int32)
    spot = jnp.arange(groups * GROUP, dtype=jnp.int32)
    found = jnp.where(place[None, :] == spot[:, None], slot[None, :] * 128 + cols[None, :], -1)
    found = jnp.max(found, axis=1)
    block = jnp.where(found < 0, slots // 2, found // 256)
    column = jnp.where(found < 0, 0, found % 128)
    group = jnp.arange(groups, dtype=jnp.int32)
    group_row = count(ends[None, :] <= group[:, None], 1) % row_tiles
    return block, column, group_row


def tile_copies(tiles_hbm, tiles, sems):
    chunk = tiles_hbm.shape[0] // CHUNKS
    return [
        pltpu.make_async_copy(
            tiles_hbm.at[pl.ds(i * chunk, chunk)], tiles.at[pl.ds(i * chunk, chunk)], sems.at[i]
        )
        for i in range(CHUNKS)
    ]


def fill_table(table, parts, weight):
    part_tiles, _, depth = parts[0].shape
    step = 8
    for i, part in enumerate(parts):

        def some(k, carry):
            rows = part[pl.ds(k * step, step)].reshape(step * TILE, depth)
            made = jnp.dot(rows, weight[...], preferred_element_type=jnp.float32)
            made = made.astype(table.dtype).reshape(step, TILE, table.shape[2])
            table[pl.ds(i * part_tiles + k * step, step)] = made
            return carry

        lax.fori_loop(0, part_tiles // step, some, 0)


def add_groups(first, last, block, column, group_row, tiles, table, total):
    left = lax.broadcasted_iota(jnp.int32, (TILE, 2 * TILE), 1) < TILE

    def step(i, carry):
        terms = []
        for j in range(UNROLL):
            spots = [(i * UNROLL + j) * GROUP + t for t in range(GROUP)]
            lhs = [
                jnp.where(left, tiles[block[spots[t]]], tiles[block[spots[t + 1]]])
                for t in range(0, GROUP, 2)
            ]
            rhs = [table[column[spot]] for spot in spots]
            terms.append(
                jnp.dot(
                    jnp.concatenate(lhs, axis=1),
                    jnp.concatenate(rhs, axis=0),
                    preferred_element_type=jnp.float32,
                )
            )
        for j in range(UNROLL):
            total[group_row[i * UNROLL + j]] += terms[j]
        return carry

    lax.fori_loop(first, last, step, 0)


def spmm_kernel(late, block, column, group_row, steps, weight, *refs):
    n_parts = len(refs) - (7 if late else 5)
    parts, tiles_hbm, refs = refs[:n_parts], refs[n_parts], refs[n_parts + 1 :]
    if late:
        before, out, table, tiles, total, sems = refs
    else:
        total, table, tiles, sems = refs
    copies = tile_copies(tiles_hbm, tiles, sems)
    for copy in copies:
        copy.start()
    tiles[tiles_hbm.shape[0]] = jnp.zeros(tiles.shape[1:], tiles.dtype)
    total[...] = before[...] if late else jnp.zeros_like(total)
    fill_table(table, parts, weight)
    for copy in copies:
        copy.wait()
    first, last = (steps[0], steps[1]) if late else (0, steps[0])
    add_groups(first, last, block, column, group_row, tiles, table, total)
    if late:
        out[...] = total[...].reshape(out.shape).astype(out.dtype)


def spmm(plan, weight, parts, tiles, row_tiles, before=None):
    width = weight.shape[1]
    scalar = pl.BlockSpec(memory_space=pltpu.SMEM)
    vmem = pl.BlockSpec(memory_space=pltpu.VMEM)
    anywhere = pl.BlockSpec(memory_space=pl.ANY)
    sums = (row_tiles, TILE, width)
    scratch = [
        pltpu.VMEM((len(parts) * parts[0].shape[0], TILE, width), jnp.bfloat16),
        pltpu.VMEM((tiles.shape[0] + 1, *tiles.shape[1:]), tiles.dtype),
    ]
    late = before is not None
    if late:
        scratch.append(pltpu.VMEM(sums, jnp.float32))
        out = jax.ShapeDtypeStruct((row_tiles * TILE, width), jnp.bfloat16)
    else:
        out = jax.ShapeDtypeStruct(sums, jnp.float32)
    return pl.pallas_call(
        functools.partial(spmm_kernel, late),
        out_shape=out,
        in_specs=[scalar] * len(plan) + [vmem] * (1 + len(parts)) + [anywhere] + [vmem] * late,
        out_specs=vmem,
        scratch_shapes=scratch + [pltpu.SemaphoreType.DMA((CHUNKS,))],
        compiler_params=pltpu.CompilerParams(vmem_limit_bytes=SPMM_VMEM),
        name="late_groups" if late else "early_groups",
    )(*plan, weight, *parts, tiles, *([before] if late else []))


SPMM_VMEM = 46 << 20


def body(features, weight, tiles, tile_rows, tile_cols, counts):
    own, width = features.shape
    n_col = lax.axis_size("col")
    row_tiles = n_col * own // TILE
    own_tiles = own // TILE
    me = lax.axis_index("row")
    my_y, my_x = me // (X_CHIPS * CORES), me // CORES % X_CHIPS

    def part(value):
        return both_cores(value).reshape(-1, TILE, width)

    owner, inner = tile_cols[0, 0] // own_tiles, tile_cols[0, 0] % own_tiles
    y, x, core = owner // (X_CHIPS * CORES), owner // CORES % X_CHIPS, owner % CORES
    back_y, back_x = (my_y - y) % Y_CHIPS, (my_x - x) % X_CHIPS
    late = back_x % 2
    cols = ((back_x // 2 ^ late) * CORES + core) * Y_CHIPS * own_tiles
    cols = cols + back_y * own_tiles + inner

    pieces = [features] + [shift(features, k, 0) for k in (1, 2, 3)]
    places = (cols, *place_slots(tile_rows[0, 0], late, counts[0, 0], row_tiles))
    *pieces, cols, place, ends, steps = lax.optimization_barrier((*pieces, *places))
    line = jnp.concatenate(pieces, axis=0)
    across = shift(line, 0, 2)

    own_line, line, cols, place, ends = lax.optimization_barrier(
        (part(line), line, cols, place, ends)
    )
    behind, ahead = shift(line, 0, 1), shift(line, 0, 3)
    groups = fill_groups(place, ends, cols, row_tiles)
    across, *groups = lax.optimization_barrier((across, *groups))

    plan = (*groups, steps)
    early = spmm(plan, weight, [own_line, part(across)], tiles[0, 0], row_tiles)
    early, ahead = lax.optimization_barrier((early, ahead))
    late_parts = [part(ahead), part(behind)]
    partial_rows = spmm(plan, weight, late_parts, tiles[0, 0], row_tiles, early)

    received = lax.all_to_all(partial_rows, "col", 0, 0, tiled=True)
    received = received.reshape(n_col, own, width).astype(jnp.float32)
    return jnp.maximum(jnp.sum(received, axis=0), 0.0).astype(jnp.bfloat16)


def solution(mesh):
    return jax.shard_map(
        body,
        mesh=mesh,
        in_specs=(
            P(("row", "col"), None),
            P(),
            P("row", "col", None, None, None),
            P("row", "col", None),
            P("row", "col", None),
            P("row", "col"),
        ),
        out_specs=P(("row", "col"), None),
        check_vma=False,
    )
```

time: 121 us -> 113 us (0.934)
  blocking collectives: 79.4 us -> 69.9 us
  waiting for transfers between devices: 5.43 us -> 0.77 us
  Pallas kernels: 6.82 us -> 11 us
  between operations: 0.83 us -> 2.6 us
  other arithmetic: 4.16 us -> 5.58 us
    all_to_all x1, blocking collectives: 70 us -> 60.4 us  [body(): received = lax.all_to_all(partial_rows, 'col', 0, 0, tiled=True)]
    ppermute x6, waiting for transfers between devices: 5.43 us -> 0.77 us  [shift(): return lax.ppermute(value, 'row', pairs)]
    pallas_call x1 -> x2, Pallas kernels: 6.82 us -> 11 us  [spmm(): pl.pallas_call(functools.partial(spmm_kernel, late), out_shape=out, in_sp...]
  transfers between devices with their start and end apart: 6 -> 6, of which waited for: 3 -> 1; matrix products, arithmetic and copies ran while one was open for 3% -> 4% of each run, Pallas kernels for 0% -> 5%
where the time goes in v4:
time: 113 us
  blocking collectives  69.9 us (62%)
  starting transfers between devices  21.8 us (19%)
  Pallas kernels  11 us (10%)
  other arithmetic  5.58 us (5%)
  between operations  2.6 us (2%)
    all_to_all x1, blocking collectives, body(): received = lax.all_to_all(partial_rows, 'col', 0, 0, tiled=True)  60.4 us
    ppermute x6, starting transfers between devices, shift(): return lax.ppermute(value, 'row', pairs)  21.8 us
    pallas_call x2, Pallas kernels, spmm(): pl.pallas_call(functools.partial(spmm_kernel, late), out_shape=out, in_sp...  11 us
    all_gather x4, blocking collectives, both_cores(): lax.all_gather(value, 'row', axis_index_groups=groups, axis=0, tiled=True)  9.45 us
  transfers between devices with their start and end apart: 6, of which 1 were waited for; matrix products, arithmetic and copies ran while one was open for 4% of the time, Pallas kernels for 5%

profile of v4, /device:TPU:20, one launch (start us, length us, event | category | flops | bytes accessed | tf_op | source)
XLA Modules:
  0.0 112.5 jit_solution(10852056813006133391)
XLA Ops:
  0.0 0.0 copy-start
  0.0 2.4 %collective-permute-start.1 = (bf16[192,256]{1,0:T(8,128)(2,1)}, bf16[192,256]{1,0:T(8,128)(2,1)S(1)}, u32[]{:S(2)}, u32[]{:S(2)}) collective-permute-start(bf16[192,256]{1,0:T(8,128)(2,1)} %param.6), channel_id=1, source_target_pairs={{0,256},{16,272},{32,288},{48,304},{64,320},{80,336},{96,352},{112... | collective-permute-start | bytes 294920 | tf_op jit(solution)/shard_map/ppermute | solution.py:23
  2.4 3.5 %collective-permute-start = (bf16[192,256]{1,0:T(8,128)(2,1)}, bf16[192,256]{1,0:T(8,128)(2,1)S(1)}, u32[]{:S(2)}, u32[]{:S(2)}) collective-permute-start(bf16[192,256]{1,0:T(8,128)(2,1)} %param.6), channel_id=1, source_target_pairs={{0,128},{16,144},{32,160},{48,176},{64,192},{80,208},{96,224},{112... | collective-permute-start | bytes 294920 | tf_op jit(solution)/shard_map/ppermute | solution.py:23
  5.9 3.0 %collective-permute-start.2 = (bf16[192,256]{1,0:T(8,128)(2,1)}, bf16[192,256]{1,0:T(8,128)(2,1)S(1)}, u32[]{:S(2)}, u32[]{:S(2)}) collective-permute-start(bf16[192,256]{1,0:T(8,128)(2,1)} %param.6), channel_id=1, source_target_pairs={{0,384},{16,400},{32,416},{48,432},{64,448},{80,464},{96,480},{112... | collective-permute-start | bytes 294920 | tf_op jit(solution)/shard_map/ppermute | solution.py:23
  9.0 0.7 compare_reduce_fusion
  9.7 0.7 broadcast_divide_fusion
  11.0 0.7 fusion.21
  11.8 0.2 convert_reduce_fusion.1
  12.0 0.2 convert_reduce_fusion.2
  12.2 0.6 fusion.26
  14.0 0.1 select_reduce_fusion.2
  14.1 0.6 fusion.27
  15.3 0.1 select_reduce_fusion.1
  15.5 0.1 pad_add_fusion.steps
  15.6 0.0 collective-permute-done.1
  15.6 0.0 collective-permute-done
  15.6 0.0 collective-permute-done.2
  15.6 0.9 constant_dynamic-update-slice_fusion.3
  16.5 7.1 %collective-permute-start.3 = (bf16[768,256]{1,0:T(8,128)(2,1)S(1)}, bf16[768,256]{1,0:T(8,128)(2,1)S(1)}, u32[]{:S(2)}, u32[]{:S(2)}) collective-permute-start(bf16[768,256]{1,0:T(8,128)(2,1)S(1)} %constant_dynamic-update-slice_fusion), channel_id=1, source_target_pairs={{0,64},{16,80},{32,96},{48,112},{64,0},{80,16},{96,32},{112,48},{1... | collective-permute-start | bytes 1179656 | tf_op jit(solution)/shard_map/ppermute | solution.py:23
  23.6 2.4 %all_gather.12 = bf16[1536,256]{1,0:T(8,128)(2,1)S(1)} all-gather(bf16[768,256]{1,0:T(8,128)(2,1)S(1)} %constant_dynamic-update-slice_fusion), channel_id=1, replica_groups={{0,16},{32,48},{64,80},{96,112},{128,144},{160,176},{192,208},{224,240}..., dimensions={0}, use_global_device_ids=true | all-gather | bytes 1179648 | tf_op jit(solution)/shard_map/all_gather | solution.py:28
  26.0 1.9 %collective-permute-start.5 = (bf16[768,256]{1,0:T(8,128)(2,1)S(1)}, bf16[768,256]{1,0:T(8,128)(2,1)S(1)}, u32[]{:S(2)}, u32[]{:S(2)}) collective-permute-start(bf16[768,256]{1,0:T(8,128)(2,1)S(1)} %constant_dynamic-update-slice_fusion), channel_id=1, source_target_pairs={{0,32},{16,48},{32,64},{48,80},{64,96},{80,112},{96,0},{112,16},{1... | collective-permute-start | bytes 1179656 | tf_op jit(solution)/shard_map/ppermute | solution.py:23
  27.9 3.9 %collective-permute-start.4 = (bf16[768,256]{1,0:T(8,128)(2,1)S(1)}, bf16[768,256]{1,0:T(8,128)(2,1)S(1)}, u32[]{:S(2)}, u32[]{:S(2)}) collective-permute-start(bf16[768,256]{1,0:T(8,128)(2,1)S(1)} %constant_dynamic-update-slice_fusion), channel_id=1, source_target_pairs={{0,96},{16,112},{32,0},{48,16},{64,32},{80,48},{96,64},{112,80},{1... | collective-permute-start | bytes 1179656 | tf_op jit(solution)/shard_map/ppermute | solution.py:23
  31.9 0.4 select_reduce_fusion
  32.3 0.1 convert_reduce_fusion.4
  32.4 0.0 collective-permute-done.3
  32.4 2.4 %all_gather.13 = bf16[1536,256]{1,0:T(8,128)(2,1)S(1)} all-gather(bf16[768,256]{1,0:T(8,128)(2,1)S(1)} %collective-permute-done.3), channel_id=1, replica_groups={{0,16},{32,48},{64,80},{96,112},{128,144},{160,176},{192,208},{224,240}..., dimensions={0}, use_global_device_ids=true | all-gather | bytes 1179648 | tf_op jit(solution)/shard_map/all_gather | solution.py:28
  34.8 0.0 copy-done
  34.8 5.4 %early_groups.1.refs_3_ = f32[48,64,256]{2,1,0:T(8,128)S(1)} custom-call(s32[1248]{0:T(1024)S(1)} %get-tuple-element.34.block, s32[1248]{0:T(1024)S(1)} %get-tuple-element.35.column, s32[312]{0:T(512)S(1)} %add_select_fusion.2.group_row, s32[2]{0:T(128)S(1)} %pad_add_fusion.steps, bf16[256,256]{1,0:T(8,128)(2,1)S(1)} %copy-done, ...), custom_call_target="tpu_custom_call" | custom-call | tf_op jit(solution)/shard_map/early_groups/pallas_call | solution.py:160
  40.2 0.8 collective-permute-done.4
  41.0 2.4 %all_gather.14 = bf16[1536,256]{1,0:T(8,128)(2,1)S(1)} all-gather(bf16[768,256]{1,0:T(8,128)(2,1)S(1)} %collective-permute-done.4), channel_id=1, replica_groups={{0,16},{32,48},{64,80},{96,112},{128,144},{160,176},{192,208},{224,240}..., dimensions={0}, use_global_device_ids=true | all-gather | bytes 1179648 | tf_op jit(solution)/shard_map/all_gather | solution.py:28
  43.3 0.0 collective-permute-done.5
  43.3 2.4 %all_gather.15 = bf16[1536,256]{1,0:T(8,128)(2,1)S(1)} all-gather(bf16[768,256]{1,0:T(8,128)(2,1)S(1)} %collective-permute-done.5), channel_id=1, replica_groups={{0,16},{32,48},{64,80},{96,112},{128,144},{160,176},{192,208},{224,240}..., dimensions={0}, use_global_device_ids=true | all-gather | bytes 1179648 | tf_op jit(solution)/shard_map/all_gather | solution.py:28
  45.7 5.6 %late_groups.1 = bf16[3072,256]{1,0:T(8,128)(2,1)S(1)} custom-call(s32[1248]{0:T(1024)S(1)} %get-tuple-element.34.block, s32[1248]{0:T(1024)S(1)} %get-tuple-element.35.column, s32[312]{0:T(512)S(1)} %add_select_fusion.2.group_row, s32[2]{0:T(128)S(1)} %pad_add_fusion.steps, bf16[256,256]{1,0:T(8,128)(2,1)S(1)} %copy-done, ...), custom_call_target="tpu_custom_call" | custom-call | tf_op jit(solution)/shard_map/late_groups/pallas_call | solution.py:160
  51.3 60.4 %all_to_all.9 = bf16[16,192,256]{2,1,0:T(8,128)(2,1)S(1)} all-to-all(bf16[16,192,256]{2,1,0:T(8,128)(2,1)S(1)} %bitcast.14), channel_id=1, replica_groups=mesh['row'=32,'col'=16] {'col'}, dimensions={0} | all-to-all | bytes 3145728 | tf_op jit(solution)/shard_map/all_to_all | solution.py:211
  111.7 0.2 convert_reduce_fusion
  111.9 0.7 maximum_convert_fusion
  (9 shorter events, 0.1 us)
Async XLA Ops:
  0.0 34.8 %copy-start = (bf16[256,256]{1,0:T(8,128)(2,1)S(1)}, bf16[256,256]{1,0:T(8,128)(2,1)}, u32[]{:S(2)}) copy-start(bf16[256,256]{1,0:T(8,128)(2,1)} %weight.3) | copy-start | bytes 393220
  0.0 15.6 %collective-permute-start.1 = (bf16[192,256]{1,0:T(8,128)(2,1)}, bf16[192,256]{1,0:T(8,128)(2,1)S(1)}, u32[]{:S(2)}, u32[]{:S(2)}) collective-permute-start(bf16[192,256]{1,0:T(8,128)(2,1)} %param.6), channel_id=1, source_target_pairs={{0,256},{16,272},{32,288},{48,304},{64,320},{80,336},{96,352},{112... | collective-permute-start | bytes 294920 | tf_op jit(solution)/shard_map/ppermute | solution.py:23
  2.4 13.2 %collective-permute-start = (bf16[192,256]{1,0:T(8,128)(2,1)}, bf16[192,256]{1,0:T(8,128)(2,1)S(1)}, u32[]{:S(2)}, u32[]{:S(2)}) collective-permute-start(bf16[192,256]{1,0:T(8,128)(2,1)} %param.6), channel_id=1, source_target_pairs={{0,128},{16,144},{32,160},{48,176},{64,192},{80,208},{96,224},{112... | collective-permute-start | bytes 294920 | tf_op jit(solution)/shard_map/ppermute | solution.py:23
  5.9 9.7 %collective-permute-start.2 = (bf16[192,256]{1,0:T(8,128)(2,1)}, bf16[192,256]{1,0:T(8,128)(2,1)S(1)}, u32[]{:S(2)}, u32[]{:S(2)}) collective-permute-start(bf16[192,256]{1,0:T(8,128)(2,1)} %param.6), channel_id=1, source_target_pairs={{0,384},{16,400},{32,416},{48,432},{64,448},{80,464},{96,480},{112... | collective-permute-start | bytes 294920 | tf_op jit(solution)/shard_map/ppermute | solution.py:23
  16.5 15.9 %collective-permute-start.3 = (bf16[768,256]{1,0:T(8,128)(2,1)S(1)}, bf16[768,256]{1,0:T(8,128)(2,1)S(1)}, u32[]{:S(2)}, u32[]{:S(2)}) collective-permute-start(bf16[768,256]{1,0:T(8,128)(2,1)S(1)} %constant_dynamic-update-slice_fusion), channel_id=1, source_target_pairs={{0,64},{16,80},{32,96},{48,112},{64,0},{80,16},{96,32},{112,48},{1... | collective-permute-start | bytes 1179656 | tf_op jit(solution)/shard_map/ppermute | solution.py:23
  26.0 17.3 %collective-permute-start.5 = (bf16[768,256]{1,0:T(8,128)(2,1)S(1)}, bf16[768,256]{1,0:T(8,128)(2,1)S(1)}, u32[]{:S(2)}, u32[]{:S(2)}) collective-permute-start(bf16[768,256]{1,0:T(8,128)(2,1)S(1)} %constant_dynamic-update-slice_fusion), channel_id=1, source_target_pairs={{0,32},{16,48},{32,64},{48,80},{64,96},{80,112},{96,0},{112,16},{1... | collective-permute-start | bytes 1179656 | tf_op jit(solution)/shard_map/ppermute | solution.py:23
  27.9 13.1 %collective-permute-start.4 = (bf16[768,256]{1,0:T(8,128)(2,1)S(1)}, bf16[768,256]{1,0:T(8,128)(2,1)S(1)}, u32[]{:S(2)}, u32[]{:S(2)}) collective-permute-start(bf16[768,256]{1,0:T(8,128)(2,1)S(1)} %constant_dynamic-update-slice_fusion), channel_id=1, source_target_pairs={{0,96},{16,112},{32,0},{48,16},{64,32},{80,48},{96,64},{112,80},{1... | collective-permute-start | bytes 1179656 | tf_op jit(solution)/shard_map/ppermute | solution.py:23

commit v5 on v4

--- a/solution.py
+++ b/solution.py
@@ -28,45 +28,94 @@
     return lax.all_gather(value, "row", axis_index_groups=groups, axis=0, tiled=True)
 
 
-def count(mask, axis):
-    return jnp.sum(mask.astype(jnp.int32), axis=axis)
-
-
-def place_slots(rows, late, live, row_tiles):
+def plan_kernel(own_tiles, row_tiles, me, live, rows_hbm, cols_hbm, own_hbm, *refs):
+    block, column, group_row, steps, own, rows_ref, cols_ref, sems = refs
+    copies = [
+        pltpu.make_async_copy(source, target, sems.at[i])
+        for i, (source, target) in enumerate(
+            ((rows_hbm, rows_ref), (cols_hbm, cols_ref), (own_hbm, own))
+        )
+    ]
+    for copy in copies:
+        copy.start()
+    for copy in copies:
+        copy.wait()
+    slots = rows_ref.shape[1]
     keys = 2 * row_tiles
-    slot = jnp.arange(rows.shape[0], dtype=jnp.int32)
-    odd = slot % 2
-    key = jnp.where(slot < live, late * row_tiles + rows, keys)
-    full_key = key * 2 + odd
-    rank = count((full_key[None, :] == full_key[:, None]) & (slot[None, :] < slot[:, None]), 1)
-    key_id = jnp.arange(keys, dtype=jnp.int32)
-    evens = count(full_key[None, :] == 2 * key_id[:, None], 1)
-    odds = count(full_key[None, :] == 2 * key_id[:, None] + 1, 1)
-    held = (jnp.maximum(evens, odds) + 1) // 2
-    early = jnp.sum(jnp.where(key_id < row_tiles, held, 0))
-    early_steps = (early + UNROLL - 1) // UNROLL
-    gap = early_steps * UNROLL - early
-    skip = jnp.where(key_id < row_tiles, 0, gap)
-    ends = jnp.sum(jnp.where(key_id[None, :] <= key_id[:, None], held[None, :], 0), axis=1) + skip
-    base = jnp.sum(jnp.where(key_id[None, :] < key[:, None], held[None, :], 0), axis=1)
-    base = base + jnp.where(key < row_tiles, 0, gap)
-    place = jnp.where(slot < live, base * GROUP + rank * 2 + odd, -1)
-    return place, ends, jnp.stack([early_steps, (jnp.max(ends) + UNROLL - 1) // UNROLL])
-
-
-def fill_groups(place, ends, cols, row_tiles):
-    slots = place.shape[0]
-    groups = (slots + ends.shape[0]) // 2 + UNROLL - 1
-    groups = (groups + UNROLL - 1) // UNROLL * UNROLL
-    slot = jnp.arange(slots, dtype=jnp.int32)
-    spot = jnp.arange(groups * GROUP, dtype=jnp.int32)
-    found = jnp.where(place[None, :] == spot[:, None], slot[None, :] * 128 + cols[None, :], -1)
-    found = jnp.max(found, axis=1)
-    block = jnp.where(found < 0, slots // 2, found // 256)
-    column = jnp.where(found < 0, 0, found % 128)
-    group = jnp.arange(groups, dtype=jnp.int32)
-    group_row = count(ends[None, :] <= group[:, None], 1) % row_tiles
-    return block, column, group_row
+
+    def iota(rows, lanes, axis):
+        return lax.broadcasted_iota(jnp.int32, (rows, lanes), axis)
+
+    def ones(mask):
+        return jnp.where(mask, 1.0, 0.0)
+
+    slot = iota(1, slots, 1)
+    odd = slot & 1
+    alive = slot < live[0, 0]
+    owner = (cols_ref[...] * (128 // own_tiles + 1)) >> 7
+    inner = cols_ref[...] - owner * own_tiles
+    y, x, core = owner // (X_CHIPS * CORES), owner // CORES % X_CHIPS, owner % CORES
+    back_y, back_x = (me[0] - y) % Y_CHIPS, (me[1] - x) % X_CHIPS
+    late = back_x % 2
+    col = ((back_x // 2 ^ late) * CORES + core) * Y_CHIPS * own_tiles + back_y * own_tiles + inner
+    key = jnp.where(alive, late * row_tiles + rows_ref[...], keys)
+
+    match = key == iota(keys, slots, 0)
+    is_odd = jnp.broadcast_to(odd, (keys, slots)) == 1
+    odds = ones(match & is_odd)
+    evens = ones(match) - odds
+    most = jnp.maximum(jnp.sum(evens, axis=1, keepdims=True), jnp.sum(odds, axis=1, keepdims=True))
+    held = (most.astype(jnp.int32) + 1) >> 1
+    held = jnp.broadcast_to(held, (keys, 128)).astype(jnp.float32)
+    upto = ones(iota(keys, keys, 1) <= iota(keys, keys, 0)).astype(jnp.bfloat16)
+    ends = jnp.dot(upto, held.astype(jnp.bfloat16), preferred_element_type=jnp.float32)
+    early = ends[row_tiles - 1 : row_tiles].astype(jnp.int32)
+    early_steps = (early + UNROLL - 1) >> UNROLL.bit_length() - 1
+    gap = (early_steps * UNROLL - early).astype(jnp.float32)
+    ends = ends + jnp.where(iota(keys, 128, 0) < row_tiles, 0.0, gap)
+    base = ends - held
+    last_steps = (ends[keys - 1 :].astype(jnp.int32) + UNROLL - 1) >> UNROLL.bit_length() - 1
+    steps[...] = jnp.where(iota(1, 128, 1) == 0, early_steps, last_steps)
+
+    before = ones(iota(slots, slots, 0) < iota(slots, slots, 1)).astype(jnp.bfloat16)
+    even_rank = jnp.dot(evens.astype(jnp.bfloat16), before, preferred_element_type=jnp.float32)
+    odd_rank = jnp.dot(odds.astype(jnp.bfloat16), before, preferred_element_type=jnp.float32)
+    spots = (evens + odds) * base[:, :1] * GROUP + (evens * even_rank + odds * odd_rank) * 2
+    place = jnp.sum(spots, axis=0, keepdims=True).astype(jnp.int32) + odd
+    place = jnp.where(alive, place, -1)
+
+    n_spots = block.shape[1]
+    taken = ones(place == iota(n_spots, slots, 0)).astype(jnp.bfloat16)
+    line = iota(8, slots, 0)
+    values = jnp.where(line == 0, slot // 2, jnp.where(line == 1, col, jnp.where(line == 2, 1, 0)))
+    values = values.astype(jnp.float32).astype(jnp.bfloat16)
+    found = lax.dot_general(
+        values, taken, (((1,), (1,)), ((), ())), preferred_element_type=jnp.float32
+    )
+    block[...] = jnp.where(found[2:3] > 0.5, found[:1], float(slots // 2)).astype(jnp.int32)
+    column[...] = found[1:2].astype(jnp.int32)
+    n_groups = group_row.shape[1]
+    passed = ones(ends[:, :1] <= iota(keys, n_groups, 1).astype(jnp.float32))
+    row = jnp.sum(passed, axis=0, keepdims=True).astype(jnp.int32)
+    row = jnp.where(row < row_tiles, row, row - row_tiles)
+    group_row[...] = jnp.where(row < row_tiles, row, 0)
+
+
+def plan(rows, cols, live, me, own, row_tiles):
+    groups = (rows.shape[1] + 2 * row_tiles) // 2 + UNROLL - 1
+    spots = (groups * GROUP + 127) // 128 * 128
+    scalar = pl.BlockSpec(memory_space=pltpu.SMEM)
+    vmem = pl.BlockSpec(memory_space=pltpu.VMEM)
+    return pl.pallas_call(
+        functools.partial(plan_kernel, own.shape[0] // TILE, row_tiles),
+        out_shape=[jax.ShapeDtypeStruct((1, n), jnp.int32) for n in (spots, spots, 384, 128)]
+        + [jax.ShapeDtypeStruct(own.shape, own.dtype)],
+        in_specs=[scalar] * 2 + [pl.BlockSpec(memory_space=pl.ANY)] * 3,
+        out_specs=[vmem] * 5,
+        scratch_shapes=[pltpu.VMEM(rows.shape, jnp.int32)] * 2 + [pltpu.SemaphoreType.DMA((3,))],
+        compiler_params=pltpu.CompilerParams(vmem_limit_bytes=40 << 20),
+        name="plan",
+    )(me, live, rows, cols, own)
 
 
 def tile_copies(tiles_hbm, tiles, sems):
@@ -102,10 +151,10 @@
         for j in range(UNROLL):
             spots = [(i * UNROLL + j) * GROUP + t for t in range(GROUP)]
             lhs = [
-                jnp.where(left, tiles[block[spots[t]]], tiles[block[spots[t + 1]]])
+                jnp.where(left, tiles[block[0, spots[t]]], tiles[block[0, spots[t + 1]]])
                 for t in range(0, GROUP, 2)
             ]
-            rhs = [table[column[spot]] for spot in spots]
+            rhs = [table[column[0, spot]] for spot in spots]
             terms.append(
                 jnp.dot(
                     jnp.concatenate(lhs, axis=1),
@@ -114,7 +163,7 @@
                 )
             )
         for j in range(UNROLL):
-            total[group_row[i * UNROLL + j]] += terms[j]
+            total[group_row[0, i * UNROLL + j]] += terms[j]
         return carry
 
     lax.fori_loop(first, last, step, 0)
@@ -135,7 +184,7 @@
     fill_table(table, parts, weight)
     for copy in copies:
         copy.wait()
-    first, last = (steps[0], steps[1]) if late else (0, steps[0])
+    first, last = (steps[0, 0], steps[0, 1]) if late else (0, steps[0, 0])
     add_groups(first, last, block, column, group_row, tiles, table, total)
     if late:
         out[...] = total[...].reshape(out.shape).astype(out.dtype)
@@ -175,38 +224,28 @@
     own, width = features.shape
     n_col = lax.axis_size("col")
     row_tiles = n_col * own // TILE
-    own_tiles = own // TILE
     me = lax.axis_index("row")
     my_y, my_x = me // (X_CHIPS * CORES), me // CORES % X_CHIPS
 
     def part(value):
         return both_cores(value).reshape(-1, TILE, width)
 
-    owner, inner = tile_cols[0, 0] // own_tiles, tile_cols[0, 0] % own_tiles
-    y, x, core = owner // (X_CHIPS * CORES), owner // CORES % X_CHIPS, owner % CORES
-    back_y, back_x = (my_y - y) % Y_CHIPS, (my_x - x) % X_CHIPS
-    late = back_x % 2
-    cols = ((back_x // 2 ^ late) * CORES + core) * Y_CHIPS * own_tiles
-    cols = cols + back_y * own_tiles + inner
-
-    pieces = [features] + [shift(features, k, 0) for k in (1, 2, 3)]
-    places = (cols, *place_slots(tile_rows[0, 0], late, counts[0, 0], row_tiles))
-    *pieces, cols, place, ends, steps = lax.optimization_barrier((*pieces, *places))
+    pieces = [shift(features, k, 0) for k in (1, 2, 3)]
+    place = jnp.stack([my_y, my_x]).astype(jnp.int32)
+    *groups, own_rows = plan(tile_rows[0], tile_cols[0], counts, place, features, row_tiles)
+    *pieces, block, column, group_row, steps = lax.optimization_barrier(
+        (own_rows, *pieces, *groups)
+    )
     line = jnp.concatenate(pieces, axis=0)
     across = shift(line, 0, 2)
-
-    own_line, line, cols, place, ends = lax.optimization_barrier(
-        (part(line), line, cols, place, ends)
-    )
+    own_line, line = lax.optimization_barrier((part(line), line))
     behind, ahead = shift(line, 0, 1), shift(line, 0, 3)
-    groups = fill_groups(place, ends, cols, row_tiles)
-    across, *groups = lax.optimization_barrier((across, *groups))
-
-    plan = (*groups, steps)
-    early = spmm(plan, weight, [own_line, part(across)], tiles[0, 0], row_tiles)
+
+    groups = (block, column, group_row, steps)
+    early = spmm(groups, weight, [own_line, part(across)], tiles[0, 0], row_tiles)
     early, ahead = lax.optimization_barrier((early, ahead))
     late_parts = [part(ahead), part(behind)]
-    partial_rows = spmm(plan, weight, late_parts, tiles[0, 0], row_tiles, early)
+    partial_rows = spmm(groups, weight, late_parts, tiles[0, 0], row_tiles, early)
 
     received = lax.all_to_all(partial_rows, "col", 0, 0, tiled=True)
     received = received.reshape(n_col, own, width).astype(jnp.float32)

time: 113 us -> 118 us (1.044)
  the two profiles are of different devices: /device:TPU:20 before, /device:TPU:16 now
where the time goes in v5:
time: 118 us
  blocking collectives  77.9 us (66%)
  starting transfers between devices  23.1 us (20%)
  Pallas kernels  11.4 us (10%)
  local copies, waits for them, and re-layouts  2.29 us (2%)
    all_to_all x1, blocking collectives, body(): received = lax.all_to_all(partial_rows, 'col', 0, 0, tiled=True)  67.1 us
    ppermute x6, starting transfers between devices, shift(): return lax.ppermute(value, 'row', pairs)  23.1 us
    all_gather x4, blocking collectives, both_cores(): lax.all_gather(value, 'row', axis_index_groups=groups, axis=0, tiled=True)  10.8 us
    pallas_call x2, Pallas kernels, spmm(): pl.pallas_call(functools.partial(spmm_kernel, late), out_shape=out, in_sp...  9.72 us
  transfers between devices with their start and end apart: 6, of which 1 were waited for; matrix products, arithmetic and copies ran while one was open for 0% of the time, Pallas kernels for 5%

profile of v5, /device:TPU:16, one launch (start us, length us, event | category | flops | bytes accessed | tf_op | source)
XLA Modules:
  0.0 117.5 jit_solution(8940163297133028182)
XLA Ops:
  0.0 0.0 copy-start
  0.0 3.6 %collective-permute-start = (bf16[192,256]{1,0:T(8,128)(2,1)}, bf16[192,256]{1,0:T(8,128)(2,1)S(1)}, u32[]{:S(2)}, u32[]{:S(2)}) collective-permute-start(bf16[192,256]{1,0:T(8,128)(2,1)} %own_hbm.1), channel_id=1, source_target_pairs={{0,128},{16,144},{32,160},{48,176},{64,192},{80,208},{96,224},{112... | collective-permute-start | bytes 294920 | tf_op jit(solution)/shard_map/ppermute | solution.py:23
  3.6 2.4 %collective-permute-start.2 = (bf16[192,256]{1,0:T(8,128)(2,1)}, bf16[192,256]{1,0:T(8,128)(2,1)S(1)}, u32[]{:S(2)}, u32[]{:S(2)}) collective-permute-start(bf16[192,256]{1,0:T(8,128)(2,1)} %own_hbm.1), channel_id=1, source_target_pairs={{0,384},{16,400},{32,416},{48,432},{64,448},{80,464},{96,480},{112... | collective-permute-start | bytes 294920 | tf_op jit(solution)/shard_map/ppermute | solution.py:23
  6.0 9.4 %collective-permute-start.1 = (bf16[192,256]{1,0:T(8,128)(2,1)}, bf16[192,256]{1,0:T(8,128)(2,1)S(1)}, u32[]{:S(2)}, u32[]{:S(2)}) collective-permute-start(bf16[192,256]{1,0:T(8,128)(2,1)} %own_hbm.1), channel_id=1, source_target_pairs={{0,256},{16,272},{32,288},{48,304},{64,320},{80,336},{96,352},{112... | collective-permute-start | bytes 294920 | tf_op jit(solution)/shard_map/ppermute | solution.py:23
  16.1 0.1 pad_add_fusion.me
  16.2 0.0 copy-start.1
  16.2 0.9 copy-done.1
  17.1 0.0 copy-start.2
  17.1 0.7 copy-done.2
  17.7 0.0 copy-start.3
  17.7 0.7 copy-done.3
  18.4 1.7 %plan.1 = (s32[1,1280]{1,0:T(1,128)S(1)}, s32[1,1280]{1,0:T(1,128)S(1)}, s32[1,384]{1,0:T(1,128)S(1)}, s32[1,128]{1,0:T(1,128)S(1)}, bf16[192,256]{1,0:T(8,128)(2,1)S(1)}) custom-call(s32[2]{0:T(128)S(1)} %pad_add_fusion.me, s32[1,1]{1,0:T(1,128)S(6)} %copy.10.live, s32[1,512]{1,0:T(1,128)S(1)} %bitcast.15, s32[1,512]{1,0:T(1,128)S(1)} %bitcast.16, ...), custom_call_target="tpu_custom_call" | custom-call | tf_op jit(solution)/shard_map/plan/pallas_call | solution.py:109
  20.1 0.0 collective-permute-done
  20.1 0.0 collective-permute-done.2
  20.1 0.0 collective-permute-done.1
  20.2 1.9 %collective-permute-start.3 = (bf16[768,256]{1,0:T(8,128)(2,1)S(1)}, bf16[768,256]{1,0:T(8,128)(2,1)S(1)}, u32[]{:S(2)}, u32[]{:S(2)}) collective-permute-start(bf16[768,256]{1,0:T(8,128)(2,1)S(1)} %constant_dynamic-update-slice_fusion), channel_id=1, source_target_pairs={{0,64},{16,80},{32,96},{48,112},{64,0},{80,16},{96,32},{112,48},{1... | collective-permute-start | bytes 1179656 | tf_op jit(solution)/shard_map/ppermute | solution.py:23
  22.1 2.4 %all_gather.12 = bf16[1536,256]{1,0:T(8,128)(2,1)S(1)} all-gather(bf16[768,256]{1,0:T(8,128)(2,1)S(1)} %constant_dynamic-update-slice_fusion), channel_id=1, replica_groups={{0,16},{32,48},{64,80},{96,112},{128,144},{160,176},{192,208},{224,240}..., dimensions={0}, use_global_device_ids=true | all-gather | bytes 1179648 | tf_op jit(solution)/shard_map/all_gather | solution.py:28
  24.5 1.9 %collective-permute-start.4 = (bf16[768,256]{1,0:T(8,128)(2,1)S(1)}, bf16[768,256]{1,0:T(8,128)(2,1)S(1)}, u32[]{:S(2)}, u32[]{:S(2)}) collective-permute-start(bf16[768,256]{1,0:T(8,128)(2,1)S(1)} %constant_dynamic-update-slice_fusion), channel_id=1, source_target_pairs={{0,96},{16,112},{32,0},{48,16},{64,32},{80,48},{96,64},{112,80},{1... | collective-permute-start | bytes 1179656 | tf_op jit(solution)/shard_map/ppermute | solution.py:23
  26.4 3.9 %collective-permute-start.5 = (bf16[768,256]{1,0:T(8,128)(2,1)S(1)}, bf16[768,256]{1,0:T(8,128)(2,1)S(1)}, u32[]{:S(2)}, u32[]{:S(2)}) collective-permute-start(bf16[768,256]{1,0:T(8,128)(2,1)S(1)} %constant_dynamic-update-slice_fusion), channel_id=1, source_target_pairs={{0,32},{16,48},{32,64},{48,80},{64,96},{80,112},{96,0},{112,16},{1... | collective-permute-start | bytes 1179656 | tf_op jit(solution)/shard_map/ppermute | solution.py:23
  30.3 1.0 collective-permute-done.3
  31.4 2.4 %all_gather.13 = bf16[1536,256]{1,0:T(8,128)(2,1)S(1)} all-gather(bf16[768,256]{1,0:T(8,128)(2,1)S(1)} %collective-permute-done.3), channel_id=1, replica_groups={{0,16},{32,48},{64,80},{96,112},{128,144},{160,176},{192,208},{224,240}..., dimensions={0}, use_global_device_ids=true | all-gather | bytes 1179648 | tf_op jit(solution)/shard_map/all_gather | solution.py:28
  33.7 0.0 copy-done
  33.7 4.8 %early_groups.1.refs_3_ = f32[48,64,256]{2,1,0:T(8,128)S(1)} custom-call(s32[1,1280]{1,0:T(1,128)S(1)} %get-tuple-element.27.block, s32[1,1280]{1,0:T(1,128)S(1)} %get-tuple-element.28.column, s32[1,384]{1,0:T(1,128)S(1)} %get-tuple-element.29.group_row, s32[1,128]{1,0:T(1,128)S(1)} %get-tuple-element.30.steps, bf16[256,256]{1,0:T(8,128)(2,1)S(1)} %copy-done, ...), custom_call_target="tpu_custom_call" | custom-call | tf_op jit(solution)/shard_map/early_groups/pallas_call | solution.py:209
  38.5 0.0 collective-permute-done.4
  38.5 3.7 %all_gather.14 = bf16[1536,256]{1,0:T(8,128)(2,1)S(1)} all-gather(bf16[768,256]{1,0:T(8,128)(2,1)S(1)} %collective-permute-done.4), channel_id=1, replica_groups={{0,16},{32,48},{64,80},{96,112},{128,144},{160,176},{192,208},{224,240}..., dimensions={0}, use_global_device_ids=true | all-gather | bytes 1179648 | tf_op jit(solution)/shard_map/all_gather | solution.py:28
  42.2 0.0 collective-permute-done.5
  42.2 2.4 %all_gather.15 = bf16[1536,256]{1,0:T(8,128)(2,1)S(1)} all-gather(bf16[768,256]{1,0:T(8,128)(2,1)S(1)} %collective-permute-done.5), channel_id=1, replica_groups={{0,16},{32,48},{64,80},{96,112},{128,144},{160,176},{192,208},{224,240}..., dimensions={0}, use_global_device_ids=true | all-gather | bytes 1179648 | tf_op jit(solution)/shard_map/all_gather | solution.py:28
  44.6 4.9 %late_groups.1 = bf16[3072,256]{1,0:T(8,128)(2,1)S(1)} custom-call(s32[1,1280]{1,0:T(1,128)S(1)} %get-tuple-element.27.block, s32[1,1280]{1,0:T(1,128)S(1)} %get-tuple-element.28.column, s32[1,384]{1,0:T(1,128)S(1)} %get-tuple-element.29.group_row, s32[1,128]{1,0:T(1,128)S(1)} %get-tuple-element.30.steps, bf16[256,256]{1,0:T(8,128)(2,1)S(1)} %copy-done, ...), custom_call_target="tpu_custom_call" | custom-call | tf_op jit(solution)/shard_map/late_groups/pallas_call | solution.py:209
  49.5 67.1 %all_to_all.9 = bf16[16,192,256]{2,1,0:T(8,128)(2,1)S(1)} all-to-all(bf16[16,192,256]{2,1,0:T(8,128)(2,1)S(1)} %bitcast.10), channel_id=1, replica_groups=mesh['row'=32,'col'=16] {'col'}, dimensions={0} | all-to-all | bytes 3145728 | tf_op jit(solution)/shard_map/all_to_all | solution.py:250
  116.6 0.2 convert_reduce_fusion
  116.9 0.7 maximum_convert_fusion
  (4 shorter events, 0.0 us)
Async XLA Ops:
  0.0 33.7 %copy-start = (bf16[256,256]{1,0:T(8,128)(2,1)S(1)}, bf16[256,256]{1,0:T(8,128)(2,1)}, u32[]{:S(2)}) copy-start(bf16[256,256]{1,0:T(8,128)(2,1)} %weight.3) | copy-start | bytes 393220
  0.0 20.1 %collective-permute-start = (bf16[192,256]{1,0:T(8,128)(2,1)}, bf16[192,256]{1,0:T(8,128)(2,1)S(1)}, u32[]{:S(2)}, u32[]{:S(2)}) collective-permute-start(bf16[192,256]{1,0:T(8,128)(2,1)} %own_hbm.1), channel_id=1, source_target_pairs={{0,128},{16,144},{32,160},{48,176},{64,192},{80,208},{96,224},{112... | collective-permute-start | bytes 294920 | tf_op jit(solution)/shard_map/ppermute | solution.py:23
  3.6 16.5 %collective-permute-start.2 = (bf16[192,256]{1,0:T(8,128)(2,1)}, bf16[192,256]{1,0:T(8,128)(2,1)S(1)}, u32[]{:S(2)}, u32[]{:S(2)}) collective-permute-start(bf16[192,256]{1,0:T(8,128)(2,1)} %own_hbm.1), channel_id=1, source_target_pairs={{0,384},{16,400},{32,416},{48,432},{64,448},{80,464},{96,480},{112... | collective-permute-start | bytes 294920 | tf_op jit(solution)/shard_map/ppermute | solution.py:23
  6.0 14.1 %collective-permute-start.1 = (bf16[192,256]{1,0:T(8,128)(2,1)}, bf16[192,256]{1,0:T(8,128)(2,1)S(1)}, u32[]{:S(2)}, u32[]{:S(2)}) collective-permute-start(bf16[192,256]{1,0:T(8,128)(2,1)} %own_hbm.1), channel_id=1, source_target_pairs={{0,256},{16,272},{32,288},{48,304},{64,320},{80,336},{96,352},{112... | collective-permute-start | bytes 294920 | tf_op jit(solution)/shard_map/ppermute | solution.py:23
  16.2 0.9 copy-start.1
  17.1 0.7 copy-start.2
  17.7 0.7 copy-start.3
  20.2 11.2 %collective-permute-start.3 = (bf16[768,256]{1,0:T(8,128)(2,1)S(1)}, bf16[768,256]{1,0:T(8,128)(2,1)S(1)}, u32[]{:S(2)}, u32[]{:S(2)}) collective-permute-start(bf16[768,256]{1,0:T(8,128)(2,1)S(1)} %constant_dynamic-update-slice_fusion), channel_id=1, source_target_pairs={{0,64},{16,80},{32,96},{48,112},{64,0},{80,16},{96,32},{112,48},{1... | collective-permute-start | bytes 1179656 | tf_op jit(solution)/shard_map/ppermute | solution.py:23
  24.5 14.0 %collective-permute-start.4 = (bf16[768,256]{1,0:T(8,128)(2,1)S(1)}, bf16[768,256]{1,0:T(8,128)(2,1)S(1)}, u32[]{:S(2)}, u32[]{:S(2)}) collective-permute-start(bf16[768,256]{1,0:T(8,128)(2,1)S(1)} %constant_dynamic-update-slice_fusion), channel_id=1, source_target_pairs={{0,96},{16,112},{32,0},{48,16},{64,32},{80,48},{96,64},{112,80},{1... | collective-permute-start | bytes 1179656 | tf_op jit(solution)/shard_map/ppermute | solution.py:23
  26.4 15.8 %collective-permute-start.5 = (bf16[768,256]{1,0:T(8,128)(2,1)S(1)}, bf16[768,256]{1,0:T(8,128)(2,1)S(1)}, u32[]{:S(2)}, u32[]{:S(2)}) collective-permute-start(bf16[768,256]{1,0:T(8,128)(2,1)S(1)} %constant_dynamic-update-slice_fusion), channel_id=1, source_target_pairs={{0,32},{16,48},{32,64},{48,80},{64,96},{80,112},{96,0},{112,16},{1... | collective-permute-start | bytes 1179656 | tf_op jit(solution)/shard_map/ppermute | solution.py:23

commit v6 on v5

--- a/solution.py
+++ b/solution.py
@@ -9,8 +9,9 @@
 
 TILE = 64
 Y_CHIPS, X_CHIPS, CORES = 4, 4, 2
+HALVES = 2
 GROUP = 4
-UNROLL = 8
+UNROLL = 16
 CHUNKS = 4
 
 
@@ -21,6 +22,16 @@
         y, x = (y + dy) % Y_CHIPS, (x + dx) % X_CHIPS
         pairs.append((source, (y * X_CHIPS + x) * CORES + core))
     return lax.ppermute(value, "row", pairs)
+
+
+def z_neighbours(n_col, offset):
+    n_z = n_col // HALVES
+    pairs = []
+    for source in range(n_col):
+        z, half = source // HALVES, source % HALVES
+        z = (z + 1 if z % 2 == offset else z - 1) % n_z
+        pairs.append((source, z * HALVES + half))
+    return pairs
 
 
 def both_cores(value):
@@ -169,13 +180,12 @@
     lax.fori_loop(first, last, step, 0)
 
 
-def spmm_kernel(late, block, column, group_row, steps, weight, *refs):
-    n_parts = len(refs) - (7 if late else 5)
-    parts, tiles_hbm, refs = refs[:n_parts], refs[n_parts], refs[n_parts + 1 :]
+def spmm_kernel(late, block, column, group_row, steps, *refs):
     if late:
-        before, out, table, tiles, total, sems = refs
+        odd_z, weight, *parts, tiles_hbm, before = refs[:-7]
+        kept, first_half, second_half, table, tiles, total, sems = refs[-7:]
     else:
-        total, table, tiles, sems = refs
+        weight, *parts, tiles_hbm, total, table, tiles, sems = refs
     copies = tile_copies(tiles_hbm, tiles, sems)
     for copy in copies:
         copy.start()
@@ -187,10 +197,16 @@
     first, last = (steps[0, 0], steps[0, 1]) if late else (0, steps[0, 0])
     add_groups(first, last, block, column, group_row, tiles, table, total)
     if late:
-        out[...] = total[...].reshape(out.shape).astype(out.dtype)
-
-
-def spmm(plan, weight, parts, tiles, row_tiles, before=None):
+        n_pairs, per_pair, lanes = kept.shape[0], kept.shape[1], first_half.shape[3]
+        for pair in range(n_pairs):
+            here = total[pl.ds((2 * pair + odd_z[0]) * per_pair, per_pair)]
+            there = total[pl.ds((2 * pair + 1 - odd_z[0]) * per_pair, per_pair)]
+            kept[pair] = here
+            first_half[pair] = there[:, :, :lanes].astype(first_half.dtype)
+            second_half[pair] = there[:, :, lanes:].astype(second_half.dtype)
+
+
+def spmm(plan, weight, parts, tiles, row_tiles, before=None, odd_z=None, n_pairs=None):
     width = weight.shape[1]
     scalar = pl.BlockSpec(memory_space=pltpu.SMEM)
     vmem = pl.BlockSpec(memory_space=pltpu.VMEM)
@@ -201,20 +217,47 @@
         pltpu.VMEM((tiles.shape[0] + 1, *tiles.shape[1:]), tiles.dtype),
     ]
     late = before is not None
+    scalars = list(plan)
     if late:
+        scalars.append(odd_z)
         scratch.append(pltpu.VMEM(sums, jnp.float32))
-        out = jax.ShapeDtypeStruct((row_tiles * TILE, width), jnp.bfloat16)
+        out = (n_pairs, row_tiles // (2 * n_pairs), TILE)
+        half = jax.ShapeDtypeStruct((*out, width // 2), jnp.bfloat16)
+        outs = [jax.ShapeDtypeStruct((*out, width), jnp.float32), half, half]
     else:
-        out = jax.ShapeDtypeStruct(sums, jnp.float32)
+        outs = jax.ShapeDtypeStruct(sums, jnp.float32)
     return pl.pallas_call(
         functools.partial(spmm_kernel, late),
-        out_shape=out,
-        in_specs=[scalar] * len(plan) + [vmem] * (1 + len(parts)) + [anywhere] + [vmem] * late,
-        out_specs=vmem,
+        out_shape=outs,
+        in_specs=[scalar] * len(scalars)
+        + [vmem] * (1 + len(parts))
+        + [anywhere]
+        + [vmem] * late,
+        out_specs=[vmem] * 3 if late else vmem,
         scratch_shapes=scratch + [pltpu.SemaphoreType.DMA((CHUNKS,))],
         compiler_params=pltpu.CompilerParams(vmem_limit_bytes=SPMM_VMEM),
         name="late_groups" if late else "early_groups",
-    )(*plan, weight, *parts, tiles, *([before] if late else []))
+    )(*scalars, weight, *parts, tiles, *([before] if late else []))
+
+
+def merge_kernel(kept, first_half, second_half, out):
+    lanes = first_half.shape[3]
+    first = kept[:, :, :, :lanes] + first_half[...].astype(jnp.float32)
+    second = kept[:, :, :, lanes:] + second_half[...].astype(jnp.float32)
+    out[:, :, :, :lanes] = first.astype(out.dtype)
+    out[:, :, :, lanes:] = second.astype(out.dtype)
+
+
+def merge(kept, first_half, second_half):
+    vmem = pl.BlockSpec(memory_space=pltpu.VMEM)
+    return pl.pallas_call(
+        merge_kernel,
+        out_shape=jax.ShapeDtypeStruct(kept.shape, jnp.bfloat16),
+        in_specs=[vmem] * 3,
+        out_specs=vmem,
+        compiler_params=pltpu.CompilerParams(vmem_limit_bytes=SPMM_VMEM),
+        name="merge_pair",
+    )(kept, first_half, second_half)
 
 
 SPMM_VMEM = 46 << 20
@@ -245,10 +288,22 @@
     early = spmm(groups, weight, [own_line, part(across)], tiles[0, 0], row_tiles)
     early, ahead = lax.optimization_barrier((early, ahead))
     late_parts = [part(ahead), part(behind)]
-    partial_rows = spmm(groups, weight, late_parts, tiles[0, 0], row_tiles, early)
-
-    received = lax.all_to_all(partial_rows, "col", 0, 0, tiled=True)
-    received = received.reshape(n_col, own, width).astype(jnp.float32)
+    z = lax.axis_index("col") // HALVES
+    odd_z = (z % 2).reshape(1).astype(jnp.int32)
+    n_pairs = n_col // (2 * HALVES)
+    kept, first_half, second_half = spmm(
+        groups, weight, late_parts, tiles[0, 0], row_tiles, early, odd_z, n_pairs
+    )
+    first_half = lax.ppermute(first_half, "col", z_neighbours(n_col, 0))
+    second_half = lax.ppermute(second_half, "col", z_neighbours(n_col, 1))
+    sums = merge(kept, first_half, second_half).reshape(-1, width)
+
+    groups = [
+        [(2 * pair + odd) * HALVES + half for pair in range(n_pairs) for half in range(HALVES)]
+        for odd in range(2)
+    ]
+    received = lax.all_to_all(sums, "col", 0, 0, axis_index_groups=groups, tiled=True)
+    received = received.reshape(len(groups[0]), own, width).astype(jnp.float32)
     return jnp.maximum(jnp.sum(received, axis=0), 0.0).astype(jnp.bfloat16)
 
 

time: 118 us -> 111 us (0.941)
  the two profiles are of different devices: /device:TPU:16 before, /device:TPU:2 now
where the time goes in v6:
time: 111 us; the launch traced here: 110 us
  blocking collectives  46.7 us (42%)
  starting transfers between devices  35.1 us (32%)
  Pallas kernels  13.9 us (13%)
  waiting for transfers between devices  10.6 us (10%)
  local copies, waits for them, and re-layouts  2.29 us (2%)
    all_to_all x1, blocking collectives, body(): lax.all_to_all(sums, 'col', 0, 0, axis_index_groups=groups, tiled=True)  37.2 us
    ppermute x6, starting transfers between devices, shift(): return lax.ppermute(value, 'row', pairs)  22.5 us
    pallas_call x2, Pallas kernels, spmm(): pl.pallas_call(functools.partial(spmm_kernel, late), out_shape=outs, in_s...  12.1 us
    all_gather x4, blocking collectives, both_cores(): lax.all_gather(value, 'row', axis_index_groups=groups, axis=0, tiled=True)  9.46 us
    ppermute x1, waiting for transfers between devices, body(): second_half = lax.ppermute(second_half, 'col', z_neighbours(n_col, 1))  8.6 us
    ppermute x1, starting transfers between devices, body(): second_half = lax.ppermute(second_half, 'col', z_neighbours(n_col, 1))  8.59 us
    ppermute x1, starting transfers between devices, body(): first_half = lax.ppermute(first_half, 'col', z_neighbours(n_col, 0))  4.01 us
    unnamed x11, local copies, waits for them, and re-layouts  2.28 us
  transfers between devices with their start and end apart: 8, of which 3 were waited for; matrix products, arithmetic and copies ran while one was open for 0% of the time, Pallas kernels for 7%

profile of v6, /device:TPU:2, one launch (start us, length us, event | category | flops | bytes accessed | tf_op | source)
XLA Modules:
  0.0 110.3 jit_solution(7492644894787296615)
XLA Ops:
  0.0 0.0 copy-start
  0.0 3.6 %collective-permute-start = (bf16[192,256]{1,0:T(8,128)(2,1)}, bf16[192,256]{1,0:T(8,128)(2,1)S(1)}, u32[]{:S(2)}, u32[]{:S(2)}) collective-permute-start(bf16[192,256]{1,0:T(8,128)(2,1)} %own_hbm.1), channel_id=1, source_target_pairs={{0,128},{16,144},{32,160},{48,176},{64,192},{80,208},{96,224},{112... | collective-permute-start | bytes 294920 | tf_op jit(solution)/shard_map/ppermute | solution.py:24
  3.6 4.2 %collective-permute-start.2 = (bf16[192,256]{1,0:T(8,128)(2,1)}, bf16[192,256]{1,0:T(8,128)(2,1)S(1)}, u32[]{:S(2)}, u32[]{:S(2)}) collective-permute-start(bf16[192,256]{1,0:T(8,128)(2,1)} %own_hbm.1), channel_id=1, source_target_pairs={{0,384},{16,400},{32,416},{48,432},{64,448},{80,464},{96,480},{112... | collective-permute-start | bytes 294920 | tf_op jit(solution)/shard_map/ppermute | solution.py:24
  7.8 2.7 %collective-permute-start.1 = (bf16[192,256]{1,0:T(8,128)(2,1)}, bf16[192,256]{1,0:T(8,128)(2,1)S(1)}, u32[]{:S(2)}, u32[]{:S(2)}) collective-permute-start(bf16[192,256]{1,0:T(8,128)(2,1)} %own_hbm.1), channel_id=1, source_target_pairs={{0,256},{16,272},{32,288},{48,304},{64,320},{80,336},{96,352},{112... | collective-permute-start | bytes 294920 | tf_op jit(solution)/shard_map/ppermute | solution.py:24
  11.2 0.1 pad_add_fusion.me
  11.2 0.0 copy-start.1
  11.3 0.9 copy-done.1
  12.1 0.0 copy-start.2
  12.1 0.7 copy-done.2
  12.8 0.0 copy-start.3
  12.8 0.7 copy-done.3
  13.5 1.7 %plan.1 = (s32[1,1280]{1,0:T(1,128)S(1)}, s32[1,1280]{1,0:T(1,128)S(1)}, s32[1,384]{1,0:T(1,128)S(1)}, s32[1,128]{1,0:T(1,128)S(1)}, bf16[192,256]{1,0:T(8,128)(2,1)S(1)}) custom-call(s32[2]{0:T(128)S(1)} %pad_add_fusion.me, s32[1,1]{1,0:T(1,128)S(6)} %copy.10.live, s32[1,512]{1,0:T(1,128)S(1)} %bitcast.16, s32[1,512]{1,0:T(1,128)S(1)} %bitcast.17, ...), custom_call_target="tpu_custom_call" | custom-call | tf_op jit(solution)/shard_map/plan/pallas_call | solution.py:120
  15.2 0.0 collective-permute-done
  15.2 0.0 collective-permute-done.2
  15.2 1.3 %collective-permute-done.1 = bf16[192,256]{1,0:T(8,128)(2,1)S(1)} collective-permute-done((bf16[192,256]{1,0:T(8,128)(2,1)}, bf16[192,256]{1,0:T(8,128)(2,1)S(1)}, u32[]{:S(2)}, u32[]{:S(2)}) %collective-permute-start.1) | collective-permute-done | bytes 98336 | tf_op jit(solution)/shard_map/ppermute | solution.py:24
  16.5 4.0 %collective-permute-start.3 = (bf16[768,256]{1,0:T(8,128)(2,1)S(1)}, bf16[768,256]{1,0:T(8,128)(2,1)S(1)}, u32[]{:S(2)}, u32[]{:S(2)}) collective-permute-start(bf16[768,256]{1,0:T(8,128)(2,1)S(1)} %constant_dynamic-update-slice_fusion), channel_id=1, source_target_pairs={{0,64},{16,80},{32,96},{48,112},{64,0},{80,16},{96,32},{112,48},{1... | collective-permute-start | bytes 1179656 | tf_op jit(solution)/shard_map/ppermute | solution.py:24
  20.6 2.4 %all_gather.12 = bf16[1536,256]{1,0:T(8,128)(2,1)S(1)} all-gather(bf16[768,256]{1,0:T(8,128)(2,1)S(1)} %constant_dynamic-update-slice_fusion), channel_id=1, replica_groups={{0,16},{32,48},{64,80},{96,112},{128,144},{160,176},{192,208},{224,240}..., dimensions={0}, use_global_device_ids=true | all-gather | bytes 1179648 | tf_op jit(solution)/shard_map/all_gather | solution.py:39
  23.0 4.6 %collective-permute-start.4 = (bf16[768,256]{1,0:T(8,128)(2,1)S(1)}, bf16[768,256]{1,0:T(8,128)(2,1)S(1)}, u32[]{:S(2)}, u32[]{:S(2)}) collective-permute-start(bf16[768,256]{1,0:T(8,128)(2,1)S(1)} %constant_dynamic-update-slice_fusion), channel_id=1, source_target_pairs={{0,96},{16,112},{32,0},{48,16},{64,32},{80,48},{96,64},{112,80},{1... | collective-permute-start | bytes 1179656 | tf_op jit(solution)/shard_map/ppermute | solution.py:24
  27.6 3.4 %collective-permute-start.5 = (bf16[768,256]{1,0:T(8,128)(2,1)S(1)}, bf16[768,256]{1,0:T(8,128)(2,1)S(1)}, u32[]{:S(2)}, u32[]{:S(2)}) collective-permute-start(bf16[768,256]{1,0:T(8,128)(2,1)S(1)} %constant_dynamic-update-slice_fusion), channel_id=1, source_target_pairs={{0,32},{16,48},{32,64},{48,80},{64,96},{80,112},{96,0},{112,16},{1... | collective-permute-start | bytes 1179656 | tf_op jit(solution)/shard_map/ppermute | solution.py:24
  31.0 0.0 collective-permute-done.3
  31.0 2.4 %all_gather.13 = bf16[1536,256]{1,0:T(8,128)(2,1)S(1)} all-gather(bf16[768,256]{1,0:T(8,128)(2,1)S(1)} %collective-permute-done.3), channel_id=1, replica_groups={{0,16},{32,48},{64,80},{96,112},{128,144},{160,176},{192,208},{224,240}..., dimensions={0}, use_global_device_ids=true | all-gather | bytes 1179648 | tf_op jit(solution)/shard_map/all_gather | solution.py:39
  33.4 0.0 copy-done
  33.4 6.0 %early_groups.1.refs_5_ = f32[48,64,256]{2,1,0:T(8,128)S(1)} custom-call(s32[1,1280]{1,0:T(1,128)S(1)} %get-tuple-element.30.block, s32[1,1280]{1,0:T(1,128)S(1)} %get-tuple-element.31.column, s32[1,384]{1,0:T(1,128)S(1)} %get-tuple-element.32.group_row, s32[1,128]{1,0:T(1,128)S(1)} %get-tuple-element.33.steps, bf16[256,256]{1,0:T(8,128)(2,1)S(1)} %copy-done, ...), custom_call_target="tpu_custom_call" | custom-call | tf_op jit(solution)/shard_map/early_groups/pallas_call | solution.py:229
  39.3 0.0 collective-permute-done.4
  39.4 2.4 %all_gather.14 = bf16[1536,256]{1,0:T(8,128)(2,1)S(1)} all-gather(bf16[768,256]{1,0:T(8,128)(2,1)S(1)} %collective-permute-done.4), channel_id=1, replica_groups={{0,16},{32,48},{64,80},{96,112},{128,144},{160,176},{192,208},{224,240}..., dimensions={0}, use_global_device_ids=true | all-gather | bytes 1179648 | tf_op jit(solution)/shard_map/all_gather | solution.py:39
  41.7 0.0 collective-permute-done.5
  41.7 2.4 %all_gather.15 = bf16[1536,256]{1,0:T(8,128)(2,1)S(1)} all-gather(bf16[768,256]{1,0:T(8,128)(2,1)S(1)} %collective-permute-done.5), channel_id=1, replica_groups={{0,16},{32,48},{64,80},{96,112},{128,144},{160,176},{192,208},{224,240}..., dimensions={0}, use_global_device_ids=true | all-gather | bytes 1179648 | tf_op jit(solution)/shard_map/all_gather | solution.py:39
  44.1 6.1 %late_groups.1 = (f32[4,6,64,256]{3,2,1,0:T(8,128)S(1)}, bf16[4,6,64,128]{3,2,1,0:T(8,128)(2,1)S(1)}, bf16[4,6,64,128]{3,2,1,0:T(8,128)(2,1)S(1)}) custom-call(s32[1,1280]{1,0:T(1,128)S(1)} %get-tuple-element.30.block, s32[1,1280]{1,0:T(1,128)S(1)} %get-tuple-element.31.column, s32[1,384]{1,0:T(1,128)S(1)} %get-tuple-element.32.group_row, ...), custom_call_target="tpu_custom_call" | custom-call | tf_op jit(solution)/shard_map/late_groups/pallas_call | solution.py:229
  50.2 4.0 %collective-permute-start.6 = (bf16[4,6,64,128]{3,2,1,0:T(8,128)(2,1)S(1)}, bf16[4,6,64,128]{3,2,1,0:T(8,128)(2,1)S(1)}, u32[]{:S(2)}, u32[]{:S(2)}) collective-permute-start(bf16[4,6,64,128]{3,2,1,0:T(8,128)(2,1)S(1)} %get-tuple-element.43), channel_id=1, source_target_pairs={{0,2},{1,3},{2,0},{3,1},{4,6},{5,7},{6,4},{7,5},{8,10},{9,11},{10,... | collective-permute-start | bytes 1179656 | tf_op jit(solution)/shard_map/ppermute | solution.py:297
  54.2 8.6 %collective-permute-start.7 = (bf16[4,6,64,128]{3,2,1,0:T(8,128)(2,1)S(1)}, bf16[4,6,64,128]{3,2,1,0:T(8,128)(2,1)S(1)}, u32[]{:S(2)}, u32[]{:S(2)}) collective-permute-start(bf16[4,6,64,128]{3,2,1,0:T(8,128)(2,1)S(1)} %get-tuple-element.44), channel_id=1, source_target_pairs={{0,14},{1,15},{2,4},{3,5},{4,2},{5,3},{6,8},{7,9},{8,6},{9,7},{10,... | collective-permute-start | bytes 1179656 | tf_op jit(solution)/shard_map/ppermute | solution.py:298
  62.8 0.7 collective-permute-done.6.first_half
  63.5 8.6 %collective-permute-done.7.second_half = bf16[4,6,64,128]{3,2,1,0:T(8,128)(2,1)S(1)} collective-permute-done((bf16[4,6,64,128]{3,2,1,0:T(8,128)(2,1)S(1)}, bf16[4,6,64,128]{3,2,1,0:T(8,128)(2,1)S(1)}, u32[]{:S(2)}, u32[]{:S(2)}) %collective-permute-start.7) | collective-permute-done | bytes 393248 | tf_op jit(solution)/shard_map/ppermute | solution.py:298
  72.1 0.2 merge_pair.1
  72.3 37.2 %all_to_all.9 = bf16[8,192,256]{2,1,0:T(8,128)(2,1)S(1)} all-to-all(bf16[8,192,256]{2,1,0:T(8,128)(2,1)S(1)} %bitcast.15), channel_id=1, replica_groups={{0,1,4,5,8,9,12,13},{2,3,6,7,10,11,14,15},{16,17,20,21,24,25,28,29},{18..., dimensions={0} | all-to-all | bytes 1572864 | tf_op jit(solution)/shard_map/all_to_all | solution.py:305
  109.6 0.1 convert_reduce_fusion
  109.7 0.7 maximum_convert_fusion
  (4 shorter events, 0.0 us)
Async XLA Ops:
  0.0 33.4 %copy-start = (bf16[256,256]{1,0:T(8,128)(2,1)S(1)}, bf16[256,256]{1,0:T(8,128)(2,1)}, u32[]{:S(2)}) copy-start(bf16[256,256]{1,0:T(8,128)(2,1)} %refs_1_.1) | copy-start | bytes 393220
  0.0 15.2 %collective-permute-start = (bf16[192,256]{1,0:T(8,128)(2,1)}, bf16[192,256]{1,0:T(8,128)(2,1)S(1)}, u32[]{:S(2)}, u32[]{:S(2)}) collective-permute-start(bf16[192,256]{1,0:T(8,128)(2,1)} %own_hbm.1), channel_id=1, source_target_pairs={{0,128},{16,144},{32,160},{48,176},{64,192},{80,208},{96,224},{112... | collective-permute-start | bytes 294920 | tf_op jit(solution)/shard_map/ppermute | solution.py:24
  3.6 11.6 %collective-permute-start.2 = (bf16[192,256]{1,0:T(8,128)(2,1)}, bf16[192,256]{1,0:T(8,128)(2,1)S(1)}, u32[]{:S(2)}, u32[]{:S(2)}) collective-permute-start(bf16[192,256]{1,0:T(8,128)(2,1)} %own_hbm.1), channel_id=1, source_target_pairs={{0,384},{16,400},{32,416},{48,432},{64,448},{80,464},{96,480},{112... | collective-permute-start | bytes 294920 | tf_op jit(solution)/shard_map/ppermute | solution.py:24
  7.8 8.7 %collective-permute-start.1 = (bf16[192,256]{1,0:T(8,128)(2,1)}, bf16[192,256]{1,0:T(8,128)(2,1)S(1)}, u32[]{:S(2)}, u32[]{:S(2)}) collective-permute-start(bf16[192,256]{1,0:T(8,128)(2,1)} %own_hbm.1), channel_id=1, source_target_pairs={{0,256},{16,272},{32,288},{48,304},{64,320},{80,336},{96,352},{112... | collective-permute-start | bytes 294920 | tf_op jit(solution)/shard_map/ppermute | solution.py:24
  11.2 0.9 copy-start.1
  12.1 0.7 copy-start.2
  12.8 0.7 copy-start.3
  16.5 14.4 %collective-permute-start.3 = (bf16[768,256]{1,0:T(8,128)(2,1)S(1)}, bf16[768,256]{1,0:T(8,128)(2,1)S(1)}, u32[]{:S(2)}, u32[]{:S(2)}) collective-permute-start(bf16[768,256]{1,0:T(8,128)(2,1)S(1)} %constant_dynamic-update-slice_fusion), channel_id=1, source_target_pairs={{0,64},{16,80},{32,96},{48,112},{64,0},{80,16},{96,32},{112,48},{1... | collective-permute-start | bytes 1179656 | tf_op jit(solution)/shard_map/ppermute | solution.py:24
  23.0 16.4 %collective-permute-start.4 = (bf16[768,256]{1,0:T(8,128)(2,1)S(1)}, bf16[768,256]{1,0:T(8,128)(2,1)S(1)}, u32[]{:S(2)}, u32[]{:S(2)}) collective-permute-start(bf16[768,256]{1,0:T(8,128)(2,1)S(1)} %constant_dynamic-update-slice_fusion), channel_id=1, source_target_pairs={{0,96},{16,112},{32,0},{48,16},{64,32},{80,48},{96,64},{112,80},{1... | collective-permute-start | bytes 1179656 | tf_op jit(solution)/shard_map/ppermute | solution.py:24
  27.6 14.1 %collective-permute-start.5 = (bf16[768,256]{1,0:T(8,128)(2,1)S(1)}, bf16[768,256]{1,0:T(8,128)(2,1)S(1)}, u32[]{:S(2)}, u32[]{:S(2)}) collective-permute-start(bf16[768,256]{1,0:T(8,128)(2,1)S(1)} %constant_dynamic-update-slice_fusion), channel_id=1, source_target_pairs={{0,32},{16,48},{32,64},{48,80},{64,96},{80,112},{96,0},{112,16},{1... | collective-permute-start | bytes 1179656 | tf_op jit(solution)/shard_map/ppermute | solution.py:24
  50.2 13.3 %collective-permute-start.6 = (bf16[4,6,64,128]{3,2,1,0:T(8,128)(2,1)S(1)}, bf16[4,6,64,128]{3,2,1,0:T(8,128)(2,1)S(1)}, u32[]{:S(2)}, u32[]{:S(2)}) collective-permute-start(bf16[4,6,64,128]{3,2,1,0:T(8,128)(2,1)S(1)} %get-tuple-element.43), channel_id=1, source_target_pairs={{0,2},{1,3},{2,0},{3,1},{4,6},{5,7},{6,4},{7,5},{8,10},{9,11},{10,... | collective-permute-start | bytes 1179656 | tf_op jit(solution)/shard_map/ppermute | solution.py:297
  54.2 17.9 %collective-permute-start.7 = (bf16[4,6,64,128]{3,2,1,0:T(8,128)(2,1)S(1)}, bf16[4,6,64,128]{3,2,1,0:T(8,128)(2,1)S(1)}, u32[]{:S(2)}, u32[]{:S(2)}) collective-permute-start(bf16[4,6,64,128]{3,2,1,0:T(8,128)(2,1)S(1)} %get-tuple-element.44), channel_id=1, source_target_pairs={{0,14},{1,15},{2,4},{3,5},{4,2},{5,3},{6,8},{7,9},{8,6},{9,7},{10,... | collective-permute-start | bytes 1179656 | tf_op jit(solution)/shard_map/ppermute | solution.py:298

commit v7 on v6

--- a/solution.py
+++ b/solution.py
@@ -103,8 +103,9 @@
     found = lax.dot_general(
         values, taken, (((1,), (1,)), ((), ())), preferred_element_type=jnp.float32
     )
-    block[...] = jnp.where(found[2:3] > 0.5, found[:1], float(slots // 2)).astype(jnp.int32)
-    column[...] = found[1:2].astype(jnp.int32)
+    block[...] = found[:1].astype(jnp.int32)
+    empty = float(own_tiles * Y_CHIPS * CORES * 2)
+    column[...] = jnp.where(found[2:3] > 0.5, found[1:2], empty).astype(jnp.int32)
     n_groups = group_row.shape[1]
     passed = ones(ends[:, :1] <= iota(keys, n_groups, 1).astype(jnp.float32))
     row = jnp.sum(passed, axis=0, keepdims=True).astype(jnp.int32)
@@ -182,16 +183,18 @@
 
 def spmm_kernel(late, block, column, group_row, steps, *refs):
     if late:
-        odd_z, weight, *parts, tiles_hbm, before = refs[:-7]
-        kept, first_half, second_half, table, tiles, total, sems = refs[-7:]
+        odd_z, weight, *parts, tiles, before = refs[:-5]
+        kept, first_half, second_half, table, total = refs[-5:]
+        copies = []
     else:
         weight, *parts, tiles_hbm, total, table, tiles, sems = refs
-    copies = tile_copies(tiles_hbm, tiles, sems)
+        copies = tile_copies(tiles_hbm, tiles, sems)
     for copy in copies:
         copy.start()
-    tiles[tiles_hbm.shape[0]] = jnp.zeros(tiles.shape[1:], tiles.dtype)
     total[...] = before[...] if late else jnp.zeros_like(total)
     fill_table(table, parts, weight)
+    last_tile = table.shape[0] - 1
+    table[last_tile] = jnp.zeros(table.shape[1:], table.dtype)
     for copy in copies:
         copy.wait()
     first, last = (steps[0, 0], steps[0, 1]) if late else (0, steps[0, 0])
@@ -212,10 +215,7 @@
     vmem = pl.BlockSpec(memory_space=pltpu.VMEM)
     anywhere = pl.BlockSpec(memory_space=pl.ANY)
     sums = (row_tiles, TILE, width)
-    scratch = [
-        pltpu.VMEM((len(parts) * parts[0].shape[0], TILE, width), jnp.bfloat16),
-        pltpu.VMEM((tiles.shape[0] + 1, *tiles.shape[1:]), tiles.dtype),
-    ]
+    scratch = [pltpu.VMEM((len(parts) * parts[0].shape[0] + 1, TILE, width), jnp.bfloat16)]
     late = before is not None
     scalars = list(plan)
     if late:
@@ -225,17 +225,17 @@
         half = jax.ShapeDtypeStruct((*out, width // 2), jnp.bfloat16)
         outs = [jax.ShapeDtypeStruct((*out, width), jnp.float32), half, half]
     else:
+        scratch += [pltpu.VMEM(tiles.shape, tiles.dtype), pltpu.SemaphoreType.DMA((CHUNKS,))]
         outs = jax.ShapeDtypeStruct(sums, jnp.float32)
     return pl.pallas_call(
         functools.partial(spmm_kernel, late),
         out_shape=outs,
         in_specs=[scalar] * len(scalars)
         + [vmem] * (1 + len(parts))
-        + [anywhere]
-        + [vmem] * late,
+        + ([vmem] * 2 if late else [anywhere]),
         out_specs=[vmem] * 3 if late else vmem,
-        scratch_shapes=scratch + [pltpu.SemaphoreType.DMA((CHUNKS,))],
-        compiler_params=pltpu.CompilerParams(vmem_limit_bytes=SPMM_VMEM),
+        scratch_shapes=scratch,
+        compiler_params=pltpu.CompilerParams(vmem_limit_bytes=LATE_VMEM if late else SPMM_VMEM),
         name="late_groups" if late else "early_groups",
     )(*scalars, weight, *parts, tiles, *([before] if late else []))
 
@@ -261,6 +261,7 @@
 
 
 SPMM_VMEM = 46 << 20
+LATE_VMEM = 24 << 20
 
 
 def body(features, weight, tiles, tile_rows, tile_cols, counts):

time: 111 us -> 109 us (0.982)
  starting transfers between devices: 35.1 us -> 38.5 us
  Pallas kernels: 13.9 us -> 11.8 us
  blocking collectives: 46.7 us -> 45 us
    ppermute x1, starting transfers between devices: 8.59 us -> 11 us  [body(): second_half = lax.ppermute(second_half, 'col', z_neighbours(n_col, 1))]
    pallas_call x2, Pallas kernels: 12.1 us -> 9.99 us  [spmm(): pl.pallas_call(functools.partial(spmm_kernel, late), out_shape=outs, in_s...]
    all_to_all x1, blocking collectives: 37.2 us -> 35.5 us  [body(): lax.all_to_all(sums, 'col', 0, 0, axis_index_groups=groups, tiled=True)]
    unnamed x11 -> x13, local copies, waits for them, and re-layouts: 2.28 us -> 2.29 us
  transfers between devices with their start and end apart: 8 -> 8, of which waited for: 3 -> 3; matrix products, arithmetic and copies ran while one was open for 0% -> 0% of each run, Pallas kernels for 7% -> 6%
where the time goes in v7:
time: 109 us
  blocking collectives  45 us (41%)
  starting transfers between devices  38.5 us (35%)
  Pallas kernels  11.8 us (11%)
  waiting for transfers between devices  9.59 us (9%)
  local copies, waits for them, and re-layouts  2.3 us (2%)
    all_to_all x1, blocking collectives, body(): lax.all_to_all(sums, 'col', 0, 0, axis_index_groups=groups, tiled=True)  35.5 us
    ppermute x6, starting transfers between devices, shift(): return lax.ppermute(value, 'row', pairs)  22.5 us
    ppermute x1, starting transfers between devices, body(): second_half = lax.ppermute(second_half, 'col', z_neighbours(n_col, 1))  11 us
    pallas_call x2, Pallas kernels, spmm(): pl.pallas_call(functools.partial(spmm_kernel, late), out_shape=outs, in_s...  9.99 us
    all_gather x4, blocking collectives, both_cores(): lax.all_gather(value, 'row', axis_index_groups=groups, axis=0, tiled=True)  9.45 us
    ppermute x1, waiting for transfers between devices, body(): second_half = lax.ppermute(second_half, 'col', z_neighbours(n_col, 1))  7.78 us
    ppermute x1, starting transfers between devices, body(): first_half = lax.ppermute(first_half, 'col', z_neighbours(n_col, 0))  5.02 us
    unnamed x13, local copies, waits for them, and re-layouts  2.29 us
  transfers between devices with their start and end apart: 8, of which 3 were waited for; matrix products, arithmetic and copies ran while one was open for 0% of the time, Pallas kernels for 6%

profile of v7, /device:TPU:2, one launch (start us, length us, event | category | flops | bytes accessed | tf_op | source)
XLA Modules:
  0.0 108.8 jit_solution(6002934300085656730)
XLA Ops:
  0.0 0.0 copy-start.1
  0.0 3.6 %collective-permute-start = (bf16[192,256]{1,0:T(8,128)(2,1)}, bf16[192,256]{1,0:T(8,128)(2,1)S(1)}, u32[]{:S(2)}, u32[]{:S(2)}) collective-permute-start(bf16[192,256]{1,0:T(8,128)(2,1)} %own_hbm.1), channel_id=1, source_target_pairs={{0,128},{16,144},{32,160},{48,176},{64,192},{80,208},{96,224},{112... | collective-permute-start | bytes 294920 | tf_op jit(solution)/shard_map/ppermute | solution.py:24
  3.6 4.2 %collective-permute-start.2 = (bf16[192,256]{1,0:T(8,128)(2,1)}, bf16[192,256]{1,0:T(8,128)(2,1)S(1)}, u32[]{:S(2)}, u32[]{:S(2)}) collective-permute-start(bf16[192,256]{1,0:T(8,128)(2,1)} %own_hbm.1), channel_id=1, source_target_pairs={{0,384},{16,400},{32,416},{48,432},{64,448},{80,464},{96,480},{112... | collective-permute-start | bytes 294920 | tf_op jit(solution)/shard_map/ppermute | solution.py:24
  7.8 2.7 %collective-permute-start.1 = (bf16[192,256]{1,0:T(8,128)(2,1)}, bf16[192,256]{1,0:T(8,128)(2,1)S(1)}, u32[]{:S(2)}, u32[]{:S(2)}) collective-permute-start(bf16[192,256]{1,0:T(8,128)(2,1)} %own_hbm.1), channel_id=1, source_target_pairs={{0,256},{16,272},{32,288},{48,304},{64,320},{80,336},{96,352},{112... | collective-permute-start | bytes 294920 | tf_op jit(solution)/shard_map/ppermute | solution.py:24
  11.2 0.1 pad_add_fusion.me
  11.2 0.0 copy-start.2
  11.3 0.9 copy-done.2
  12.1 0.0 copy-start.3
  12.1 0.7 copy-done.3
  12.8 0.0 copy-start.4
  12.8 0.7 copy-done.4
  13.5 1.7 %plan.1 = (s32[1,1280]{1,0:T(1,128)S(1)}, s32[1,1280]{1,0:T(1,128)S(1)}, s32[1,384]{1,0:T(1,128)S(1)}, s32[1,128]{1,0:T(1,128)S(1)}, bf16[192,256]{1,0:T(8,128)(2,1)S(1)}) custom-call(s32[2]{0:T(128)S(1)} %pad_add_fusion.me, s32[1,1]{1,0:T(1,128)S(6)} %copy.10.live, s32[1,512]{1,0:T(1,128)S(1)} %bitcast.18, s32[1,512]{1,0:T(1,128)S(1)} %bitcast.19, ...), custom_call_target="tpu_custom_call" | custom-call | tf_op jit(solution)/shard_map/plan/pallas_call | solution.py:121
  15.2 0.0 collective-permute-done
  15.2 0.0 collective-permute-done.2
  15.2 1.3 %collective-permute-done.1 = bf16[192,256]{1,0:T(8,128)(2,1)S(1)} collective-permute-done((bf16[192,256]{1,0:T(8,128)(2,1)}, bf16[192,256]{1,0:T(8,128)(2,1)S(1)}, u32[]{:S(2)}, u32[]{:S(2)}) %collective-permute-start.1) | collective-permute-done | bytes 98336 | tf_op jit(solution)/shard_map/ppermute | solution.py:24
  16.5 4.0 %collective-permute-start.3 = (bf16[768,256]{1,0:T(8,128)(2,1)S(1)}, bf16[768,256]{1,0:T(8,128)(2,1)S(1)}, u32[]{:S(2)}, u32[]{:S(2)}) collective-permute-start(bf16[768,256]{1,0:T(8,128)(2,1)S(1)} %constant_dynamic-update-slice_fusion), channel_id=1, source_target_pairs={{0,64},{16,80},{32,96},{48,112},{64,0},{80,16},{96,32},{112,48},{1... | collective-permute-start | bytes 1179656 | tf_op jit(solution)/shard_map/ppermute | solution.py:24
  20.6 2.4 %all_gather.12 = bf16[1536,256]{1,0:T(8,128)(2,1)S(1)} all-gather(bf16[768,256]{1,0:T(8,128)(2,1)S(1)} %constant_dynamic-update-slice_fusion), channel_id=1, replica_groups={{0,16},{32,48},{64,80},{96,112},{128,144},{160,176},{192,208},{224,240}..., dimensions={0}, use_global_device_ids=true | all-gather | bytes 1179648 | tf_op jit(solution)/shard_map/all_gather | solution.py:39
  23.0 4.6 %collective-permute-start.4 = (bf16[768,256]{1,0:T(8,128)(2,1)S(1)}, bf16[768,256]{1,0:T(8,128)(2,1)S(1)}, u32[]{:S(2)}, u32[]{:S(2)}) collective-permute-start(bf16[768,256]{1,0:T(8,128)(2,1)S(1)} %constant_dynamic-update-slice_fusion), channel_id=1, source_target_pairs={{0,96},{16,112},{32,0},{48,16},{64,32},{80,48},{96,64},{112,80},{1... | collective-permute-start | bytes 1179656 | tf_op jit(solution)/shard_map/ppermute | solution.py:24
  27.6 3.4 %collective-permute-start.5 = (bf16[768,256]{1,0:T(8,128)(2,1)S(1)}, bf16[768,256]{1,0:T(8,128)(2,1)S(1)}, u32[]{:S(2)}, u32[]{:S(2)}) collective-permute-start(bf16[768,256]{1,0:T(8,128)(2,1)S(1)} %constant_dynamic-update-slice_fusion), channel_id=1, source_target_pairs={{0,32},{16,48},{32,64},{48,80},{64,96},{80,112},{96,0},{112,16},{1... | collective-permute-start | bytes 1179656 | tf_op jit(solution)/shard_map/ppermute | solution.py:24
  31.0 0.0 collective-permute-done.3
  31.0 2.4 %all_gather.13 = bf16[1536,256]{1,0:T(8,128)(2,1)S(1)} all-gather(bf16[768,256]{1,0:T(8,128)(2,1)S(1)} %collective-permute-done.3), channel_id=1, replica_groups={{0,16},{32,48},{64,80},{96,112},{128,144},{160,176},{192,208},{224,240}..., dimensions={0}, use_global_device_ids=true | all-gather | bytes 1179648 | tf_op jit(solution)/shard_map/all_gather | solution.py:39
  33.4 0.0 copy-done.1
  33.4 0.0 copy-start
  33.4 5.3 %early_groups.1.refs_5_ = f32[48,64,256]{2,1,0:T(8,128)S(1)} custom-call(s32[1,1280]{1,0:T(1,128)S(1)} %get-tuple-element.30.block, s32[1,1280]{1,0:T(1,128)S(1)} %get-tuple-element.31.column, s32[1,384]{1,0:T(1,128)S(1)} %get-tuple-element.32.group_row, s32[1,128]{1,0:T(1,128)S(1)} %get-tuple-element.33.steps, bf16[256,256]{1,0:T(8,128)(2,1)S(1)} %copy-done.1, ...), custom_call_target="tpu_custom_call" | custom-call | tf_op jit(solution)/shard_map/early_groups/pallas_call | solution.py:230
  38.7 0.5 collective-permute-done.4
  39.2 2.4 %all_gather.14 = bf16[1536,256]{1,0:T(8,128)(2,1)S(1)} all-gather(bf16[768,256]{1,0:T(8,128)(2,1)S(1)} %collective-permute-done.4), channel_id=1, replica_groups={{0,16},{32,48},{64,80},{96,112},{128,144},{160,176},{192,208},{224,240}..., dimensions={0}, use_global_device_ids=true | all-gather | bytes 1179648 | tf_op jit(solution)/shard_map/all_gather | solution.py:39
  41.6 0.0 collective-permute-done.5
  41.6 2.4 %all_gather.15 = bf16[1536,256]{1,0:T(8,128)(2,1)S(1)} all-gather(bf16[768,256]{1,0:T(8,128)(2,1)S(1)} %collective-permute-done.5), channel_id=1, replica_groups={{0,16},{32,48},{64,80},{96,112},{128,144},{160,176},{192,208},{224,240}..., dimensions={0}, use_global_device_ids=true | all-gather | bytes 1179648 | tf_op jit(solution)/shard_map/all_gather | solution.py:39
  44.0 0.0 copy-done
  44.0 4.6 %late_groups.1 = (f32[4,6,64,256]{3,2,1,0:T(8,128)S(1)}, bf16[4,6,64,128]{3,2,1,0:T(8,128)(2,1)S(1)}, bf16[4,6,64,128]{3,2,1,0:T(8,128)(2,1)S(1)}) custom-call(s32[1,1280]{1,0:T(1,128)S(1)} %get-tuple-element.30.block, s32[1,1280]{1,0:T(1,128)S(1)} %get-tuple-element.31.column, s32[1,384]{1,0:T(1,128)S(1)} %get-tuple-element.32.group_row, ...), custom_call_target="tpu_custom_call" | custom-call | tf_op jit(solution)/shard_map/late_groups/pallas_call | solution.py:230
  48.6 5.0 %collective-permute-start.6 = (bf16[4,6,64,128]{3,2,1,0:T(8,128)(2,1)S(1)}, bf16[4,6,64,128]{3,2,1,0:T(8,128)(2,1)S(1)}, u32[]{:S(2)}, u32[]{:S(2)}) collective-permute-start(bf16[4,6,64,128]{3,2,1,0:T(8,128)(2,1)S(1)} %get-tuple-element.43), channel_id=1, source_target_pairs={{0,2},{1,3},{2,0},{3,1},{4,6},{5,7},{6,4},{7,5},{8,10},{9,11},{10,... | collective-permute-start | bytes 1179656 | tf_op jit(solution)/shard_map/ppermute | solution.py:298
  53.6 11.0 %collective-permute-start.7 = (bf16[4,6,64,128]{3,2,1,0:T(8,128)(2,1)S(1)}, bf16[4,6,64,128]{3,2,1,0:T(8,128)(2,1)S(1)}, u32[]{:S(2)}, u32[]{:S(2)}) collective-permute-start(bf16[4,6,64,128]{3,2,1,0:T(8,128)(2,1)S(1)} %get-tuple-element.44), channel_id=1, source_target_pairs={{0,14},{1,15},{2,4},{3,5},{4,2},{5,3},{6,8},{7,9},{8,6},{9,7},{10,... | collective-permute-start | bytes 1179656 | tf_op jit(solution)/shard_map/ppermute | solution.py:299
  64.6 0.0 collective-permute-done.6.first_half
  64.6 7.8 %collective-permute-done.7.second_half = bf16[4,6,64,128]{3,2,1,0:T(8,128)(2,1)S(1)} collective-permute-done((bf16[4,6,64,128]{3,2,1,0:T(8,128)(2,1)S(1)}, bf16[4,6,64,128]{3,2,1,0:T(8,128)(2,1)S(1)}, u32[]{:S(2)}, u32[]{:S(2)}) %collective-permute-start.7) | collective-permute-done | bytes 393248 | tf_op jit(solution)/shard_map/ppermute | solution.py:299
  72.4 0.2 merge_pair.1
  72.6 35.5 %all_to_all.9 = bf16[8,192,256]{2,1,0:T(8,128)(2,1)S(1)} all-to-all(bf16[8,192,256]{2,1,0:T(8,128)(2,1)S(1)} %bitcast.17), channel_id=1, replica_groups={{0,1,4,5,8,9,12,13},{2,3,6,7,10,11,14,15},{16,17,20,21,24,25,28,29},{18..., dimensions={0} | all-to-all | bytes 1572864 | tf_op jit(solution)/shard_map/all_to_all | solution.py:306
  108.1 0.1 convert_reduce_fusion
  108.2 0.7 maximum_convert_fusion
  (4 shorter events, 0.0 us)
Async XLA Ops:
  0.0 33.4 %copy-start.1 = (bf16[256,256]{1,0:T(8,128)(2,1)S(1)}, bf16[256,256]{1,0:T(8,128)(2,1)}, u32[]{:S(2)}) copy-start(bf16[256,256]{1,0:T(8,128)(2,1)} %refs_1_.1) | copy-start | bytes 393220
  0.0 15.2 %collective-permute-start = (bf16[192,256]{1,0:T(8,128)(2,1)}, bf16[192,256]{1,0:T(8,128)(2,1)S(1)}, u32[]{:S(2)}, u32[]{:S(2)}) collective-permute-start(bf16[192,256]{1,0:T(8,128)(2,1)} %own_hbm.1), channel_id=1, source_target_pairs={{0,128},{16,144},{32,160},{48,176},{64,192},{80,208},{96,224},{112... | collective-permute-start | bytes 294920 | tf_op jit(solution)/shard_map/ppermute | solution.py:24
  3.6 11.6 %collective-permute-start.2 = (bf16[192,256]{1,0:T(8,128)(2,1)}, bf16[192,256]{1,0:T(8,128)(2,1)S(1)}, u32[]{:S(2)}, u32[]{:S(2)}) collective-permute-start(bf16[192,256]{1,0:T(8,128)(2,1)} %own_hbm.1), channel_id=1, source_target_pairs={{0,384},{16,400},{32,416},{48,432},{64,448},{80,464},{96,480},{112... | collective-permute-start | bytes 294920 | tf_op jit(solution)/shard_map/ppermute | solution.py:24
  7.8 8.7 %collective-permute-start.1 = (bf16[192,256]{1,0:T(8,128)(2,1)}, bf16[192,256]{1,0:T(8,128)(2,1)S(1)}, u32[]{:S(2)}, u32[]{:S(2)}) collective-permute-start(bf16[192,256]{1,0:T(8,128)(2,1)} %own_hbm.1), channel_id=1, source_target_pairs={{0,256},{16,272},{32,288},{48,304},{64,320},{80,336},{96,352},{112... | collective-permute-start | bytes 294920 | tf_op jit(solution)/shard_map/ppermute | solution.py:24
  11.2 0.9 copy-start.2
  12.1 0.7 copy-start.3
  12.8 0.7 copy-start.4
  16.5 14.4 %collective-permute-start.3 = (bf16[768,256]{1,0:T(8,128)(2,1)S(1)}, bf16[768,256]{1,0:T(8,128)(2,1)S(1)}, u32[]{:S(2)}, u32[]{:S(2)}) collective-permute-start(bf16[768,256]{1,0:T(8,128)(2,1)S(1)} %constant_dynamic-update-slice_fusion), channel_id=1, source_target_pairs={{0,64},{16,80},{32,96},{48,112},{64,0},{80,16},{96,32},{112,48},{1... | collective-permute-start | bytes 1179656 | tf_op jit(solution)/shard_map/ppermute | solution.py:24
  23.0 16.3 %collective-permute-start.4 = (bf16[768,256]{1,0:T(8,128)(2,1)S(1)}, bf16[768,256]{1,0:T(8,128)(2,1)S(1)}, u32[]{:S(2)}, u32[]{:S(2)}) collective-permute-start(bf16[768,256]{1,0:T(8,128)(2,1)S(1)} %constant_dynamic-update-slice_fusion), channel_id=1, source_target_pairs={{0,96},{16,112},{32,0},{48,16},{64,32},{80,48},{96,64},{112,80},{1... | collective-permute-start | bytes 1179656 | tf_op jit(solution)/shard_map/ppermute | solution.py:24
  27.6 14.0 %collective-permute-start.5 = (bf16[768,256]{1,0:T(8,128)(2,1)S(1)}, bf16[768,256]{1,0:T(8,128)(2,1)S(1)}, u32[]{:S(2)}, u32[]{:S(2)}) collective-permute-start(bf16[768,256]{1,0:T(8,128)(2,1)S(1)} %constant_dynamic-update-slice_fusion), channel_id=1, source_target_pairs={{0,32},{16,48},{32,64},{48,80},{64,96},{80,112},{96,0},{112,16},{1... | collective-permute-start | bytes 1179656 | tf_op jit(solution)/shard_map/ppermute | solution.py:24
  33.4 10.6 %copy-start = (bf16[1,1,256,64,128]{4,3,2,1,0:T(8,128)(2,1)S(1)}, bf16[1,1,256,64,128]{4,3,2,1,0:T(8,128)(2,1)}, u32[]{:S(2)}) copy-start(bf16[1,1,256,64,128]{4,3,2,1,0:T(8,128)(2,1)} %param.8) | copy-start | bytes 12582916
  48.6 16.0 %collective-permute-start.6 = (bf16[4,6,64,128]{3,2,1,0:T(8,128)(2,1)S(1)}, bf16[4,6,64,128]{3,2,1,0:T(8,128)(2,1)S(1)}, u32[]{:S(2)}, u32[]{:S(2)}) collective-permute-start(bf16[4,6,64,128]{3,2,1,0:T(8,128)(2,1)S(1)} %get-tuple-element.43), channel_id=1, source_target_pairs={{0,2},{1,3},{2,0},{3,1},{4,6},{5,7},{6,4},{7,5},{8,10},{9,11},{10,... | collective-permute-start | bytes 1179656 | tf_op jit(solution)/shard_map/ppermute | solution.py:298
  53.6 18.7 %collective-permute-start.7 = (bf16[4,6,64,128]{3,2,1,0:T(8,128)(2,1)S(1)}, bf16[4,6,64,128]{3,2,1,0:T(8,128)(2,1)S(1)}, u32[]{:S(2)}, u32[]{:S(2)}) collective-permute-start(bf16[4,6,64,128]{3,2,1,0:T(8,128)(2,1)S(1)} %get-tuple-element.44), channel_id=1, source_target_pairs={{0,14},{1,15},{2,4},{3,5},{4,2},{5,3},{6,8},{7,9},{8,6},{9,7},{10,... | collective-permute-start | bytes 1179656 | tf_op jit(solution)/shard_map/ppermute | solution.py:299
